TPU v7x, 32 devices: a whole 2x2x4 slice. The times are simulated.
32 devices in a mesh: dp: 8 (over z, y), sp: 4 (over x, core).
Axes of the slice: x: 2, y: 2, z: 4, core: 2. Of those that a mesh axis runs over, the one named last changes fastest.
Arguments:
- layer_input: bfloat16 [8, 512, 8192], P('dp', 'sp'), may hold values from -6 to 6
- value_weight: bfloat16 [8192, 512], P(('dp', 'sp')), may hold values from -0.0625 to 0.0625
- query_states: bfloat16 [8, 512, 4096], P('dp', 'sp'), may hold values from -40 to 40, as said below
- key_states: bfloat16 [8, 512, 512], P('dp', 'sp'), may hold values from -5 to 5
- out_grad: bfloat16 [8, 512, 4096], P('dp', 'sp'), may hold values from -6 to 6
- doc_ids: int32 [8, 512], P('dp', 'sp'), may hold values from 0 to 3, never falling along the last dimension, each value on 1 to 256 neighbouring positions
Outputs:
- query_grad: bfloat16 [8, 512, 4096], P('dp', 'sp')
- key_grad: bfloat16 [8, 512, 512], P('dp', 'sp')
- input_grad: bfloat16 [8, 512, 8192], P('dp', 'sp')
- value_weight_grad: float32 [8192, 512], P(('dp', 'sp'))
Inputs may be any that keep to these rules, and one draw needn't show every extreme that they name: `query_states`: queries of a head may be large multiples of keys of the same positions.
All inputs are finite; a program needn't handle non-finite values.
Results may differ from a plain program's by a relative error of at most 0.0085.
Values may be sent and summed in bfloat16 or wider, within the bound.
No kernel may reach another device: no remote copies, remote signals or barrier semaphores. Data moves between devices by JAX's collectives and lax.ppermute only.
A program may use at most 128 MiB of HBM per device.

v0:
```python
import functools
import math

import jax
import jax.numpy as jnp
from jax import lax
from jax.experimental import pallas as pl
from jax.experimental.pallas import tpu as pltpu
from jax.sharding import PartitionSpec as P

HD = 128
NEG = -1e30
BF = jnp.bfloat16
F32 = jnp.float32
NT = (((1,), (1,)), ((), ()))
TN = (((0,), (0,)), ((), ()))
NN = (((1,), (0,)), ((), ()))
MIB = 1024 * 1024
VM = pl.BlockSpec(memory_space=pltpu.VMEM)
SM = pl.BlockSpec(memory_space=pltpu.SMEM)
HB = pl.BlockSpec(memory_space=pltpu.HBM)


def dot(a, b, dims):
    return lax.dot_general(a, b, dims, preferred_element_type=F32)


def ring_order(count):
    return list(range(0, count, 2)) + list(range(1, count, 2))[::-1]


def rows_at(index, size):
    return pl.ds(pl.multiple_of(index * size, size), size)


def grant(mib):
    return pltpu.CompilerParams(vmem_limit_bytes=mib * MIB)


def column_steps(dp, width):
    return max(1, min(4, dp * width // 128 // 2))


def split_kernel(sp, steps, reps, width, base, idx_ref, x_ref, *rest):
    outs, (hold, part, sems) = rest[:sp], rest[sp:]
    block = reps * width
    copies = [
        pltpu.make_async_copy(
            x_ref.at[:, i * sp * block : (i + 1) * sp * block], hold.at[i], sems.at[i]
        )
        for i in range(steps)
    ]
    for copy in copies:
        copy.start()
    for i, copy in enumerate(copies):
        copy.wait()
        for a in range(sp):
            for d in range(reps):
                part[a, :, d * width : (d + 1) * width] = hold[
                    i, :, (d * sp + a) * width : (d * sp + a + 1) * width
                ]
        for r in range(sp):
            outs[r][:, i * block : (i + 1) * block] = part[idx_ref[base + r]]


def split_columns(idx, base, x, sp, dp, width):
    tok = x.shape[0]
    steps = column_steps(dp, width)
    reps = dp // steps
    block = reps * width
    return pl.pallas_call(
        functools.partial(split_kernel, sp, steps, reps, width, base),
        out_shape=[jax.ShapeDtypeStruct((tok, dp * width), BF)] * sp,
        in_specs=[SM, HB],
        out_specs=[VM] * sp,
        scratch_shapes=[
            pltpu.VMEM((steps, tok, sp * block), BF),
            pltpu.VMEM((sp, tok, block), BF),
            pltpu.SemaphoreType.DMA((steps,)),
        ],
        compiler_params=grant(12),
        cost_estimate=pl.CostEstimate(flops=0, bytes_accessed=4 * x.size, transcendentals=0),
        name="split_columns",
    )(idx, pltpu.with_memory_space_constraint(x, pltpu.HBM))


def join_kernel(sp, reps, width, base, idx_ref, *rest):
    ins, out, hold = rest[:sp], rest[sp], rest[sp + 1]
    block = reps * width
    at = pl.ds(pl.multiple_of(pl.program_id(0) * block, block), block)
    for r in range(sp):
        hold[idx_ref[base + r]] = ins[r][:, at]
    for a in range(sp):
        for d in range(reps):
            out[:, (d * sp + a) * width : (d * sp + a + 1) * width] = hold[
                a, :, d * width : (d + 1) * width
            ]


def join_columns(idx, base, pieces, sp, dp, width):
    tok = pieces[0].shape[0]
    steps = column_steps(dp, width)
    reps = dp // steps
    block = reps * width
    return pl.pallas_call(
        functools.partial(join_kernel, sp, reps, width, base),
        out_shape=jax.ShapeDtypeStruct((tok, sp * dp * width), BF),
        grid_spec=pltpu.PrefetchScalarGridSpec(
            num_scalar_prefetch=1,
            grid=(steps,),
            in_specs=[VM] * sp,
            out_specs=pl.BlockSpec((tok, sp * block), lambda d, _: (0, d)),
            scratch_shapes=[pltpu.VMEM((sp, tok, block), BF)],
        ),
        compiler_params=grant(12),
        cost_estimate=pl.CostEstimate(
            flops=0, bytes_accessed=4 * tok * sp * dp * width, transcendentals=0
        ),
        name="join_columns",
    )(idx, *pieces)


def block_kernel(tok, key_ref, doc_ref, out, docs, sems):
    keys = pltpu.make_async_copy(key_ref, out.at[0:tok, :], sems.at[0])
    ids = pltpu.make_async_copy(doc_ref, docs, sems.at[1])
    keys.start()
    ids.start()
    out[tok : tok + 16, :] = jnp.zeros((16, out.shape[1]), BF)
    ids.wait()
    out[tok : tok + 16, 0:tok] = jnp.broadcast_to(docs[...].astype(F32), (16, tok)).astype(BF)
    keys.wait()


def key_block(keys, docs):
    tok, kv = keys.shape
    return pl.pallas_call(
        functools.partial(block_kernel, tok),
        out_shape=jax.ShapeDtypeStruct((tok + 16, kv), BF),
        in_specs=[HB, HB],
        out_specs=VM,
        scratch_shapes=[pltpu.VMEM((1, tok), jnp.int32), pltpu.SemaphoreType.DMA((2,))],
        compiler_params=grant(4),
        cost_estimate=pl.CostEstimate(flops=0, bytes_accessed=4 * keys.size, transcendentals=0),
        name="key_block",
    )(
        pltpu.with_memory_space_constraint(keys, pltpu.HBM),
        pltpu.with_memory_space_constraint(docs, pltpu.HBM),
    )


def fill_keys(sp, tok, win, heads, idx_ref, kd_refs, key_hold, doc_hold, bias):
    first = jnp.maximum(idx_ref[0] + 1 - win, 0)
    head = pl.program_id(0)
    at = pl.ds(pl.multiple_of(head * HD, HD), HD)
    for r in range(sp):
        key_hold[rows_at(idx_ref[r], tok), :] = kd_refs[r][0:tok, at]

    @pl.when(head == 0)
    def _():
        for r in range(sp):
            doc_hold[idx_ref[r]] = kd_refs[r][tok : tok + 16, 0:tok].astype(F32)
        own = jnp.broadcast_to(doc_hold[idx_ref[0]][0:1, :], (tok, tok))
        query_at = idx_ref[0] * tok + lax.broadcasted_iota(jnp.int32, (tok, tok), 1)
        for b in range(win):
            docs = jnp.broadcast_to(doc_hold[first + b][0:1, :], (tok, tok)).T
            key_at = (first + b) * tok + lax.broadcasted_iota(jnp.int32, (tok, tok), 0)
            ok = (key_at <= query_at) & (docs == own)
            block = jnp.where(ok, F32(0.0), F32(NEG))
            for h in range(heads):
                bias[b * tok : (b + 1) * tok, h * tok : (h + 1) * tok] = block

    return first, at


def stack_heads(src, dst, tok, group):
    for h in range(group):
        dst[h * tok : (h + 1) * tok, :] = src[:, h * HD : (h + 1) * HD]


def emit_rel(acc, first, value, sp, tok, win, at, idx_ref, keep, send):
    nx = sp // 2
    acc[...] = jnp.zeros_like(acc)
    acc[pl.ds(pl.multiple_of(first * tok, tok), win * tok), :] = value
    for dx in range(nx):
        keep[dx, :, at] = acc[rows_at(idx_ref[dx], tok), :]
        send[dx, :, at] = acc[rows_at(idx_ref[nx + dx], tok), :]


def probs_kernel(sp, tok, win, group, pair, idx_ref, q_ref, g_ref, *rest):
    kds, (keep, send, lse_ref) = rest[:sp], rest[sp : sp + 3]
    key_hold, doc_hold, bias, q_st, g_st, p_st, acc = rest[sp + 3 :]
    first, cols = fill_keys(sp, tok, win, pair, idx_ref, kds, key_hold, doc_hold, bias)
    factor = F32(HD**-0.5 * math.log2(math.e))
    stack_heads(q_ref, q_st, tok, group)
    stack_heads(g_ref, g_st, tok, group)
    keys = key_hold[pl.ds(pl.multiple_of(first * tok, tok), win * tok), :]
    for h in range(0, group, pair):
        at = slice(h * tok, (h + pair) * tok)
        s = dot(keys, q_st[at, :], NT) * factor + bias[...]
        top = jnp.max(s, axis=0, keepdims=True)
        e = jnp.exp2(s - top)
        total = jnp.sum(e, axis=0, keepdims=True)
        p_st[:, at] = (e * (1.0 / total)).astype(BF)
        lse = top + jnp.log2(total)
        for i in range(pair):
            lse_ref[h + i : h + i + 1, :] = lse[:, i * tok : (i + 1) * tok]
    emit_rel(
        acc, first, dot(p_st[...], g_st[...], NN), sp, tok, win, cols, idx_ref, keep, send
    )


def probs_call(idx, q, g, kds, sp, tok, win, kvh, group):
    nx, seq, pair = sp // 2, sp * tok, 2
    part = jax.ShapeDtypeStruct((nx, tok, kvh * HD), F32)
    wide = pl.BlockSpec((tok, group * HD), lambda c, _: (0, c))
    return pl.pallas_call(
        functools.partial(probs_kernel, sp, tok, win, group, pair),
        out_shape=[part, part, jax.ShapeDtypeStruct((kvh * group, tok), F32)],
        grid_spec=pltpu.PrefetchScalarGridSpec(
            num_scalar_prefetch=1,
            grid=(kvh,),
            in_specs=[wide, wide] + [VM] * sp,
            out_specs=[VM, VM, pl.BlockSpec((group, tok), lambda c, _: (c, 0))],
            scratch_shapes=[
                pltpu.VMEM((seq, HD), BF),
                pltpu.VMEM((sp, 16, tok), F32),
                pltpu.VMEM((win * tok, pair * tok), F32),
                pltpu.VMEM((group * tok, HD), BF),
                pltpu.VMEM((group * tok, HD), BF),
                pltpu.VMEM((win * tok, group * tok), BF),
                pltpu.VMEM((seq, HD), F32),
            ],
        ),
        compiler_params=grant(20),
        cost_estimate=pl.CostEstimate(
            flops=4 * tok * win * tok * kvh * group * HD,
            bytes_accessed=8 * MIB,
            transcendentals=tok * win * tok * kvh * group,
        ),
        name="probs_dv",
    )(idx, q, g, *kds)


def scores_kernel(sp, tok, win, group, pair, idx_ref, q_ref, g_ref, lse_ref, v0_ref, v1_ref, *rest):
    nx = sp // 2
    kds, (dq_ref, keep, send) = rest[:sp], rest[sp : sp + 3]
    key_hold, doc_hold, bias, val_hold, q_st, g_st, ds_st, acc = rest[sp + 3 :]
    first, cols = fill_keys(sp, tok, win, pair, idx_ref, kds, key_hold, doc_hold, bias)
    for dx in range(nx):
        val_hold[rows_at(idx_ref[dx], tok), :] = v0_ref[dx, :, cols]
        val_hold[rows_at(idx_ref[nx + dx], tok), :] = v1_ref[dx, :, cols]
    scale = HD**-0.5
    factor = F32(scale * math.log2(math.e))
    stack_heads(q_ref, q_st, tok, group)
    stack_heads(g_ref, g_st, tok, group)
    window = pl.ds(pl.multiple_of(first * tok, tok), win * tok)
    keys, vals = key_hold[window, :], val_hold[window, :]
    for h in range(0, group, pair):
        at = slice(h * tok, (h + pair) * tok)
        lse = jnp.concatenate([lse_ref[h + i : h + i + 1, :] for i in range(pair)], axis=1)
        shift = lse - F32(math.log2(scale))
        s = dot(keys, q_st[at, :], NT) * factor + bias[...]
        scaled = jnp.exp2(s - shift)
        dp = dot(vals, g_st[at, :], NT)
        delta = jnp.sum(scaled * dp, axis=0, keepdims=True) * F32(1.0 / scale)
        ds_st[:, at] = (scaled * (dp - delta)).astype(BF)
    dq = dot(ds_st[...], keys, TN)
    for h in range(group):
        dq_ref[:, h * HD : (h + 1) * HD] = dq[h * tok : (h + 1) * tok, :].astype(BF)
    emit_rel(
        acc, first, dot(ds_st[...], q_st[...], NN), sp, tok, win, cols, idx_ref, keep, send
    )


def scores_call(idx, q, g, lse, v0, v1, kds, sp, tok, win, kvh, group):
    nx, seq, pair = sp // 2, sp * tok, 2
    part = jax.ShapeDtypeStruct((nx, tok, kvh * HD), F32)
    wide = pl.BlockSpec((tok, group * HD), lambda c, _: (0, c))
    return pl.pallas_call(
        functools.partial(scores_kernel, sp, tok, win, group, pair),
        out_shape=[jax.ShapeDtypeStruct(q.shape, BF), part, part],
        grid_spec=pltpu.PrefetchScalarGridSpec(
            num_scalar_prefetch=1,
            grid=(kvh,),
            in_specs=[wide, wide, pl.BlockSpec((group, tok), lambda c, _: (c, 0)), VM, VM]
            + [VM] * sp,
            out_specs=[wide, VM, VM],
            scratch_shapes=[
                pltpu.VMEM((seq, HD), BF),
                pltpu.VMEM((sp, 16, tok), F32),
                pltpu.VMEM((win * tok, pair * tok), F32),
                pltpu.VMEM((seq, HD), BF),
                pltpu.VMEM((group * tok, HD), BF),
                pltpu.VMEM((group * tok, HD), BF),
                pltpu.VMEM((win * tok, group * tok), BF),
                pltpu.VMEM((seq, HD), F32),
            ],
        ),
        compiler_params=grant(24),
        cost_estimate=pl.CostEstimate(
            flops=8 * tok * win * tok * kvh * group * HD,
            bytes_accessed=10 * MIB,
            transcendentals=tok * win * tok * kvh * group,
        ),
        name="scores_dq_dk",
    )(idx, q, g, lse, v0, v1, *kds)


def values_kernel(sp, dp, tok, width, base, idx_ref, *rest):
    nx = sp // 2
    xs, ws = rest[:sp], rest[sp : sp + dp]
    keep, send, x_hold, w_hold = rest[sp + dp :]
    for i in range(dp):
        w_hold[rows_at(idx_ref[base + i], width), :] = ws[i][...]
    for r in range(sp):
        x_hold[r * tok : (r + 1) * tok, :] = xs[r][...]
    out = dot(x_hold[...], w_hold[...], NN)
    for dx in range(nx):
        keep[dx] = out[dx * tok : (dx + 1) * tok]
        send[dx] = out[(nx + dx) * tok : (nx + dx + 1) * tok]


def values_call(idx, base, xs, ws, sp, dp, tok, width):
    nx, kv = sp // 2, ws[0].shape[1]
    cols = dp * width
    part = jax.ShapeDtypeStruct((nx, tok, kv), F32)
    return pl.pallas_call(
        functools.partial(values_kernel, sp, dp, tok, width, base),
        out_shape=[part, part],
        in_specs=[SM] + [VM] * (sp + dp),
        out_specs=[VM] * 2,
        scratch_shapes=[pltpu.VMEM((sp * tok, cols), BF), pltpu.VMEM((cols, kv), BF)],
        compiler_params=grant(16),
        cost_estimate=pl.CostEstimate(
            flops=2 * sp * tok * cols * kv, bytes_accessed=8 * MIB, transcendentals=0
        ),
        name="values_part",
    )(idx, *xs, *ws)


def wgrad_kernel(sp, nz, ny, tok, width, base, idx_ref, *rest):
    nx = sp // 2
    xs, (g0, g1) = rest[:sp], rest[sp : sp + 2]
    outs = rest[sp + 2 : sp + 2 + 2 * nz]
    x_hold, g_hold, total = rest[sp + 2 + 2 * nz :]
    for dx in range(nx):
        for core, src in ((0, g0), (1, g1)):
            r = core * nx + dx
            x_hold[r * tok : (r + 1) * tok, :] = xs[r][...]
            g_hold[r * tok : (r + 1) * tok, :] = src[dx]
    cols = x_hold.shape[1]
    step = min(cols, 512)
    for at in range(0, cols, step):
        total[at : at + step, :] = dot(x_hold[:, at : at + step], g_hold[...], TN)
    for k in range(nz):
        outs[k][...] = total[rows_at(idx_ref[base + k * ny], width), :].astype(BF)
        for j in range(1, ny):
            outs[nz + k][j - 1] = total[rows_at(idx_ref[base + k * ny + j], width), :]


def wgrad_call(idx, base, xs, g0, g1, sp, nz, ny, tok, width):
    kv = g0.shape[2]
    cols = nz * ny * width
    return pl.pallas_call(
        functools.partial(wgrad_kernel, sp, nz, ny, tok, width, base),
        out_shape=[jax.ShapeDtypeStruct((width, kv), BF)] * nz
        + [jax.ShapeDtypeStruct((ny - 1, width, kv), F32)] * nz,
        in_specs=[SM] + [VM] * (sp + 2),
        out_specs=[VM] * (2 * nz),
        scratch_shapes=[
            pltpu.VMEM((sp * tok, cols), BF),
            pltpu.VMEM((sp * tok, kv), BF),
            pltpu.VMEM((cols, kv), F32),
        ],
        compiler_params=grant(20),
        cost_estimate=pl.CostEstimate(
            flops=2 * sp * tok * cols * kv, bytes_accessed=7 * MIB, transcendentals=0
        ),
        name="weight_grad_part",
    )(idx, *xs, g0, g1)


def igrad_kernel(sp, dp, tok, width, base, idx_ref, g0, g1, *rest):
    nx = sp // 2
    ws, outs = rest[:dp], rest[dp : dp + sp]
    g_hold, w_hold = rest[dp + sp :]
    for i in range(dp):
        w_hold[rows_at(idx_ref[base + i], width), :] = ws[i][...]
    for dx in range(nx):
        g_hold[dx * tok : (dx + 1) * tok, :] = g0[dx]
        g_hold[(nx + dx) * tok : (nx + dx + 1) * tok, :] = g1[dx]
    cols = w_hold.shape[0]
    step = min(cols, 512)
    for at in range(0, cols, step):
        out = dot(g_hold[...], w_hold[at : at + step, :], NT)
        for r in range(sp):
            outs[r][:, at : at + step] = out[r * tok : (r + 1) * tok].astype(BF)


def igrad_call(idx, base, g0, g1, ws, sp, dp, tok, width):
    kv = g0.shape[2]
    cols = dp * width
    return pl.pallas_call(
        functools.partial(igrad_kernel, sp, dp, tok, width, base),
        out_shape=[jax.ShapeDtypeStruct((tok, cols), BF)] * sp,
        in_specs=[SM] + [VM] * (2 + dp),
        out_specs=[VM] * sp,
        scratch_shapes=[pltpu.VMEM((sp * tok, kv), BF), pltpu.VMEM((cols, kv), BF)],
        compiler_params=grant(16),
        cost_estimate=pl.CostEstimate(
            flops=2 * sp * tok * cols * kv, bytes_accessed=5 * MIB, transcendentals=0
        ),
        name="input_grad_part",
    )(idx, g0, g1, *ws)


def after(value, *others):
    return lax.optimization_barrier((value, *others))[0]


def local(layer_input, value_weight, query_states, key_states, out_grad, doc_ids):
    sp, dp = lax.axis_size("sp"), lax.axis_size("dp")
    nx = sp // 2
    ny = max(1, min(nx, dp))
    nz = dp // ny
    tok = layer_input.shape[1]
    width = value_weight.shape[0]
    kvh = key_states.shape[2] // HD
    group = query_states.shape[2] // HD // kvh
    win = min(sp, sp // 2 + 1)

    def sp_perm(dx, dc):
        return [(i, ((i // 2 + dx) % nx) * 2 + (i % 2 ^ dc)) for i in range(sp)]

    def send_sp(v, dx, dc):
        return lax.ppermute(v, "sp", sp_perm(dx % nx, dc))

    z_ring, y_ring = ring_order(nz), ring_order(ny)

    def pred(ring, at, k):
        return ring[(ring.index(at) - k) % len(ring)]

    z_next = [
        (z_ring[p] * ny + y, z_ring[(p + 1) % nz] * ny + y) for p in range(nz) for y in range(ny)
    ]
    z_back = [(j, i) for i, j in z_next]
    ahead = nz // 2
    behind = nz - 1 - ahead
    y_next = [
        (z * ny + y_ring[p], z * ny + y_ring[(p + 1) % ny]) for p in range(ny) for z in range(nz)
    ]

    def send_z(v, forward=True):
        return lax.ppermute(v, "dp", z_next if forward else z_back)

    def send_y(v):
        return lax.ppermute(v, "dp", y_next)

    from_z = [0, *range(1, ahead + 1), *(-k for k in range(1, behind + 1))]
    to_z = sorted(from_z, key=lambda k: (-abs(k), -k))

    table = []
    for d in range(dp):
        z, y = d // ny, d % ny
        for s in range(sp):
            x, core = s // 2, s % 2
            row = [((x - dx) % nx) * 2 + (core ^ dc) for dc in range(2) for dx in range(nx)]
            row += [((x + dx) % nx) * 2 + (core ^ dc) for dc in range(2) for dx in range(nx)]
            row += [
                pred(z_ring, z, k) * ny + pred(y_ring, y, j) for k in from_z for j in range(ny)
            ]
            row += [
                pred(z_ring, z, -k) * ny + pred(y_ring, y, j)
                for k in to_z
                for j in range(1, ny + 1)
            ]
            table.append(row)
    at_fwd, at_gather, at_scatter = sp, 2 * sp, 2 * sp + dp
    flat = lax.axis_index("dp") * sp + lax.axis_index("sp")
    idx = lax.dynamic_index_in_dim(jnp.asarray(table, jnp.int32), flat, 0, keepdims=False)

    q, g = query_states[0], out_grad[0]

    kd = key_block(key_states[0], doc_ids)
    near = [kd] + [send_sp(kd, dx, 0) for dx in range(1, nx)]
    kds = near + [send_sp(v, 0, 1) for v in near]

    z_rows = [value_weight]
    for _ in range(1, ahead + 1):
        z_rows.append(send_z(z_rows[-1]))
    for k in range(1, behind + 1):
        z_rows.append(send_z(z_rows[-1] if k > 1 else value_weight, False))
    rows = []
    for v in z_rows:
        for j in range(ny):
            rows.append(v)
            if j + 1 < ny:
                v = send_y(v)

    pieces = split_columns(idx, at_fwd, layer_input[0], sp, dp, width)
    ready = [pieces[0]] + [after(v, near[-1]) for v in pieces[1:]]

    dv_keep, dv_send, lse = probs_call(idx, q, g, kds, sp, tok, win, kvh, group)

    def reduce_core(keep, send):
        return keep + send_sp(send, 0, 1)

    def reduce_all(keep, send):
        here = reduce_core(keep, send)
        small = here.astype(BF)
        total, got = here, small
        for k in range(1, nx):
            got = send_sp(small, k, 0)
            total = total + jnp.roll(got, k, axis=0).astype(F32)
        mine = total.astype(BF)
        return mine, send_sp(mine, 0, 1), got

    vg0, vg1, _ = reduce_all(dv_keep, dv_send)

    xs = [pieces[0]]
    for r in range(1, sp):
        dx, dc = r % nx, r // nx
        xs.append(send_sp(ready[r], dx, dc))

    parts = igrad_call(idx, at_gather, vg0, vg1, rows, sp, dp, tok, width)

    blocks = wgrad_call(idx, at_scatter, xs, vg0, vg1, sp, nz, ny, tok, width)
    lines = {}
    for i, k in enumerate(to_z):
        line = blocks[i]
        for j in range(1, ny):
            line = send_y(line.astype(BF)).astype(F32) + blocks[nz + i][j - 1]
        lines[k] = line.astype(F32)
    weight_grad = lines[0]
    for count, sign in ((ahead, 1), (behind, -1)):
        run = None
        for k in range(count, 0, -1):
            run = lines[sign * k] if run is None else run + lines[sign * k]
            run = send_z(run.astype(BF), sign > 0).astype(F32)
        if run is not None:
            weight_grad = weight_grad + run

    v_keep, v_send = values_call(idx, at_gather, xs, rows, sp, dp, tok, width)
    v0, v1, v_got = reduce_all(v_keep, v_send)
    dq, dk_keep, dk_send = scores_call(idx, q, g, lse, v0, v1, kds, sp, tok, win, kvh, group)
    dk = reduce_core(dk_keep, dk_send)
    key_sum = dk[0]
    for k in range(1, nx):
        key_sum = key_sum + send_sp(dk[-k % nx].astype(BF), k, 0).astype(F32)
    key_grad = key_sum.astype(BF)

    back = [parts[0]]
    for r in range(1, sp):
        dx, dc = r % nx, r // nx
        if dx and dc:
            back.append(send_sp(after(parts[r], v_got), -dx, dc))
        else:
            back.append(send_sp(parts[r], -dx, dc))
    input_grad = join_columns(idx, at_fwd, back, sp, dp, width)

    return (dq[None], key_grad[None], input_grad[None], weight_grad)


def solution(mesh):
    in_specs = (
        P("dp", "sp", None),
        P(("dp", "sp"), None),
        P("dp", "sp", None),
        P("dp", "sp", None),
        P("dp", "sp", None),
        P("dp", "sp"),
    )
    out_specs = (
        P("dp", "sp", None),
        P("dp", "sp", None),
        P("dp", "sp", None),
        P(("dp", "sp"), None),
    )
    return jax.shard_map(local, mesh=mesh, in_specs=in_specs, out_specs=out_specs, check_vma=False)
```

profile of v0, /device:TPU:0, one launch (start us, length us, event | category | flops | bytes accessed | tf_op | source)
XLA Modules:
  0.0 105.1 jit_solution(8033702289493132108)
XLA Ops:
  1.6 3.0 %collective-permute-start = (bf16[144,512]{1,0:T(8,128)(2,1)S(1)}, bf16[144,512]{1,0:T(8,128)(2,1)S(1)}, u32[]{:S(2)}, u32[]{:S(2)}) collective-permute-start(bf16[144,512]{1,0:T(8,128)(2,1)S(1)} %key_block.1.rest_0_), channel_id=1, source_target_pairs={{0,2},{1,3},{2,0},{3,1},{4,6},{5,7},{6,4},{7,5},{8,10},{9,11},{10,... | collective-permute-start | bytes 442376 | tf_op jit(solution)/shard_map/ppermute | solution.py:436
  4.7 3.8 %collective-permute-done.rest_1_ = bf16[144,512]{1,0:T(8,128)(2,1)S(1)} collective-permute-done((bf16[144,512]{1,0:T(8,128)(2,1)S(1)}, bf16[144,512]{1,0:T(8,128)(2,1)S(1)}, u32[]{:S(2)}, u32[]{:S(2)}) %collective-permute-start) | collective-permute-done | bytes 147488 | tf_op jit(solution)/shard_map/ppermute | solution.py:436
  8.5 2.8 %collective-permute-start.7 = (bf16[256,512]{1,0:T(8,128)(2,1)}, bf16[256,512]{1,0:T(8,128)(2,1)S(1)}, u32[]{:S(2)}, u32[]{:S(2)}) collective-permute-start(bf16[256,512]{1,0:T(8,128)(2,1)} %rest_0_.1), channel_id=1, source_target_pairs={{0,16},{4,20},{16,24},{20,28},{24,8},{28,12},{8,0},{12,4},{1,17},{... | collective-permute-start | bytes 786440 | tf_op jit(solution)/shard_map/ppermute | solution.py:454
  12.0 1.2 %copy-done.1 = bf16[1,128,4096]{2,1,0:T(8,128)(2,1)S(1)} copy-done((bf16[1,128,4096]{2,1,0:T(8,128)(2,1)S(1)}, bf16[1,128,4096]{2,1,0:T(8,128)(2,1)}, u32[]{:S(2)}) %copy-start.1) | copy-done | bytes 1048600
  13.3 1.2 %copy-done.3 = bf16[1,128,4096]{2,1,0:T(8,128)(2,1)S(1)} copy-done((bf16[1,128,4096]{2,1,0:T(8,128)(2,1)S(1)}, bf16[1,128,4096]{2,1,0:T(8,128)(2,1)}, u32[]{:S(2)}) %copy-start.3) | copy-done | bytes 1048600
  14.5 5.0 %probs_dv.1 = (f32[2,128,512]{2,1,0:T(8,128)S(1)}, f32[2,128,512]{2,1,0:T(8,128)S(1)}, f32[32,128]{1,0:T(8,128)S(1)}) custom-call(s32[24]{0:T(128)S(1)} %dynamic-slice_bitcast_fusion.idx_ref, bf16[128,4096]{1,0:T(8,128)(2,1)S(1)} %bitcast.40, bf16[128,4096]{1,0:T(8,128)(2,1)S(1)} %bitcast.42, bf16[144,512]{1,0:T(8,128)(2,1)S(1)} %key_block.1.rest_0_, ...), custom_call_target="tpu_custom_call" | custom-call | flops 805306368 | bytes 8388608 | tf_op jit(solution)/shard_map/probs_dv/pallas_call | solution.py:216
  19.8 1.5 %collective-permute-start.6 = (bf16[256,512]{1,0:T(8,128)(2,1)S(1)}, bf16[256,512]{1,0:T(8,128)(2,1)S(1)}, u32[]{:S(2)}, u32[]{:S(2)}) collective-permute-start(bf16[256,512]{1,0:T(8,128)(2,1)S(1)} %copy-done), channel_id=1, source_target_pairs={{0,4},{8,12},{16,20},{24,28},{4,0},{12,8},{20,16},{28,24},{1,5},{9... | collective-permute-start | bytes 786440 | tf_op jit(solution)/shard_map/ppermute | solution.py:457
  21.3 2.9 %collective-permute-start.9 = (bf16[256,512]{1,0:T(8,128)(2,1)S(1)}, bf16[256,512]{1,0:T(8,128)(2,1)S(1)}, u32[]{:S(2)}, u32[]{:S(2)}) collective-permute-start(bf16[256,512]{1,0:T(8,128)(2,1)S(1)} %collective-permute-done.7.rest_6_.rest_2_), channel_id=1, source_target_pairs={{0,16},{4,20},{16,24},{20,28},{24,8},{28,12},{8,0},{12,4},{1,17},{... | collective-permute-start | bytes 786440 | tf_op jit(solution)/shard_map/ppermute | solution.py:454
  24.7 2.2 %split_columns.1 = (bf16[128,2048]{1,0:T(8,128)(2,1)S(1)}, bf16[128,2048]{1,0:T(8,128)(2,1)S(1)}, bf16[128,2048]{1,0:T(8,128)(2,1)S(1)}, bf16[128,2048]{1,0:T(8,128)(2,1)S(1)}) custom-call(s32[24]{0:T(128)S(1)} %dynamic-slice_bitcast_fusion.idx_ref, bf16[128,8192]{1,0:T(8,128)(2,1)} %bitcast.44), custom_call_target="tpu_custom_call" | custom-call | bytes 4194304 | tf_op jit(solution)/shard_map/split_columns/pallas_call | solution.py:71
  26.9 2.9 %collective-permute-done.11.rest_10_.rest_6_ = bf16[256,512]{1,0:T(8,128)(2,1)S(1)} collective-permute-done((bf16[256,512]{1,0:T(8,128)(2,1)S(1)}, bf16[256,512]{1,0:T(8,128)(2,1)S(1)}, u32[]{:S(2)}, u32[]{:S(2)}) %collective-permute-start.11) | collective-permute-done | bytes 262176 | tf_op jit(solution)/shard_map/ppermute | solution.py:454
  29.8 1.5 %collective-permute-start.3 = (bf16[128,2048]{1,0:T(8,128)(2,1)S(1)}, bf16[128,2048]{1,0:T(8,128)(2,1)S(1)}, u32[]{:S(2)}, u32[]{:S(2)}) collective-permute-start(bf16[128,2048]{1,0:T(8,128)(2,1)S(1)} %get-tuple-element.35), channel_id=1, source_target_pairs={{0,2},{1,3},{2,0},{3,1},{4,6},{5,7},{6,4},{7,5},{8,10},{9,11},{10,... | collective-permute-start | bytes 1572872 | tf_op jit(solution)/shard_map/ppermute | solution.py:436
  31.3 3.5 %collective-permute-done.9.rest_8_.rest_4_ = bf16[256,512]{1,0:T(8,128)(2,1)S(1)} collective-permute-done((bf16[256,512]{1,0:T(8,128)(2,1)S(1)}, bf16[256,512]{1,0:T(8,128)(2,1)S(1)}, u32[]{:S(2)}, u32[]{:S(2)}) %collective-permute-start.9) | collective-permute-done | bytes 262176 | tf_op jit(solution)/shard_map/ppermute | solution.py:454
  36.5 1.4 %collective-permute-start.10 = (bf16[256,512]{1,0:T(8,128)(2,1)S(1)}, bf16[256,512]{1,0:T(8,128)(2,1)S(1)}, u32[]{:S(2)}, u32[]{:S(2)}) collective-permute-start(bf16[256,512]{1,0:T(8,128)(2,1)S(1)} %collective-permute-done.9.rest_8_.rest_4_), channel_id=1, source_target_pairs={{0,4},{8,12},{16,20},{24,28},{4,0},{12,8},{20,16},{28,24},{1,5},{9... | collective-permute-start | bytes 786440 | tf_op jit(solution)/shard_map/ppermute | solution.py:457
  38.0 7.1 %collective-permute-done.12.rest_11_.rest_7_ = bf16[256,512]{1,0:T(8,128)(2,1)S(1)} collective-permute-done((bf16[256,512]{1,0:T(8,128)(2,1)S(1)}, bf16[256,512]{1,0:T(8,128)(2,1)S(1)}, u32[]{:S(2)}, u32[]{:S(2)}) %collective-permute-start.12) | collective-permute-done | bytes 262176 | tf_op jit(solution)/shard_map/ppermute | solution.py:457
  45.6 9.2 %collective-permute-done.5.rest_3_ = bf16[128,2048]{1,0:T(8,128)(2,1)S(1)} collective-permute-done((bf16[128,2048]{1,0:T(8,128)(2,1)S(1)}, bf16[128,2048]{1,0:T(8,128)(2,1)S(1)}, u32[]{:S(2)}, u32[]{:S(2)}) %collective-permute-start.5) | collective-permute-done | bytes 524320 | tf_op jit(solution)/shard_map/ppermute | solution.py:436
  54.8 1.9 %values_part.1 = (f32[2,128,512]{2,1,0:T(8,128)S(1)}, f32[2,128,512]{2,1,0:T(8,128)S(1)}) custom-call(s32[24]{0:T(128)S(1)} %dynamic-slice_bitcast_fusion.idx_ref, bf16[128,2048]{1,0:T(8,128)(2,1)S(1)} %get-tuple-element.33.rest_0_, bf16[128,2048]{1,0:T(8,128)(2,1)S(1)} %collective-permute-done.3.rest_1_, ...), custom_call_target="tpu_custom_call" | custom-call | flops 1073741824 | bytes 8388608 | tf_op jit(solution)/shard_map/values_part/pallas_call | solution.py:327
  57.7 1.6 %collective-permute-done.19 = bf16[2,128,512]{2,1,0:T(8,128)(2,1)S(1)} collective-permute-done((bf16[2,128,512]{2,1,0:T(8,128)(2,1)S(1)}, bf16[2,128,512]{2,1,0:T(8,128)(2,1)S(1)}, u32[]{:S(2)}, u32[]{:S(2)}) %collective-permute-start.19) | collective-permute-done | bytes 262176 | tf_op jit(solution)/shard_map/ppermute | solution.py:436
  59.6 1.6 %collective-permute-start.14 = (bf16[2,128,512]{2,1,0:T(8,128)(2,1)S(1)}, bf16[2,128,512]{2,1,0:T(8,128)(2,1)S(1)}, u32[]{:S(2)}, u32[]{:S(2)}) collective-permute-start(bf16[2,128,512]{2,1,0:T(8,128)(2,1)S(1)} %get-tuple-element.62), channel_id=1, source_target_pairs={{0,2},{1,3},{2,0},{3,1},{4,6},{5,7},{6,4},{7,5},{8,10},{9,11},{10,... | collective-permute-start | bytes 786440 | tf_op jit(solution)/shard_map/ppermute | solution.py:436
  61.2 2.1 %weight_grad_part.1 = (bf16[256,512]{1,0:T(8,128)(2,1)S(1)}, bf16[256,512]{1,0:T(8,128)(2,1)S(1)}, bf16[256,512]{1,0:T(8,128)(2,1)S(1)}, bf16[256,512]{1,0:T(8,1...) custom-call(s32[24]{0:T(128)S(1)} %dynamic-slice_bitcast_fusion.idx_, ...), custom_call_target="tpu_custom_call" | custom-call | flops 1073741824 | bytes 7340032 | tf_op jit(solution)/shard_map/weight_grad_part/pallas_call | solution.py:364
  63.2 1.6 %collective-permute-start.25 = (bf16[256,512]{1,0:T(8,128)(2,1)S(1)}, bf16[256,512]{1,0:T(8,128)(2,1)S(1)}, u32[]{:S(2)}, u32[]{:S(2)}) collective-permute-start(bf16[256,512]{1,0:T(8,128)(2,1)S(1)} %get-tuple-element.54), channel_id=1, source_target_pairs={{0,4},{8,12},{16,20},{24,28},{4,0},{12,8},{20,16},{28,24},{1,5},{9... | collective-permute-start | bytes 786440 | tf_op jit(solution)/shard_map/ppermute | solution.py:457
  65.3 1.5 %collective-permute-start.29 = (bf16[256,512]{1,0:T(8,128)(2,1)S(1)}, bf16[256,512]{1,0:T(8,128)(2,1)S(1)}, u32[]{:S(2)}, u32[]{:S(2)}) collective-permute-start(bf16[256,512]{1,0:T(8,128)(2,1)S(1)} %get-tuple-element.58), channel_id=1, source_target_pairs={{0,4},{8,12},{16,20},{24,28},{4,0},{12,8},{20,16},{28,24},{1,5},{9... | collective-permute-start | bytes 786440 | tf_op jit(solution)/shard_map/ppermute | solution.py:457
  66.8 1.5 %collective-permute-done.14 = bf16[2,128,512]{2,1,0:T(8,128)(2,1)S(1)} collective-permute-done((bf16[2,128,512]{2,1,0:T(8,128)(2,1)S(1)}, bf16[2,128,512]{2,1,0:T(8,128)(2,1)S(1)}, u32[]{:S(2)}, u32[]{:S(2)}) %collective-permute-start.14) | collective-permute-done | bytes 262176 | tf_op jit(solution)/shard_map/ppermute | solution.py:436
  68.6 2.0 %input_grad_part.1 = (bf16[128,2048]{1,0:T(8,128)(2,1)S(1)}, bf16[128,2048]{1,0:T(8,128)(2,1)S(1)}, bf16[128,2048]{1,0:T(8,128)(2,1)S(1)}, bf16[128,2048]{1,0:T(8,128)(2,1)S(1)}) custom-call(s32[24]{0:T(128)S(1)} %dynamic-slice_bitcast_fusion.idx_ref, bf16[2,128,512]{2,1,0:T(8,128)(2,1)S(1)} %add_convert_fusion.g0.rest_4_, ...), custom_call_target="tpu_custom_call" | custom-call | flops 1073741824 | bytes 5242880 | tf_op jit(solution)/shard_map/input_grad_part/pallas_call | solution.py:403
  70.6 1.6 %collective-permute-start.21 = (bf16[128,2048]{1,0:T(8,128)(2,1)S(1)}, bf16[128,2048]{1,0:T(8,128)(2,1)S(1)}, u32[]{:S(2)}, u32[]{:S(2)}) collective-permute-start(bf16[128,2048]{1,0:T(8,128)(2,1)S(1)} %get-tuple-element.48), channel_id=1, source_target_pairs={{0,2},{1,3},{2,0},{3,1},{4,6},{5,7},{6,4},{7,5},{8,10},{9,11},{10,... | collective-permute-start | bytes 1572872 | tf_op jit(solution)/shard_map/ppermute | solution.py:436
  73.3 6.4 %scores_dq_dk.1 = (bf16[128,4096]{1,0:T(8,128)(2,1)}, f32[2,128,512]{2,1,0:T(8,128)S(1)}, f32[2,128,512]{2,1,0:T(8,128)S(1)}) custom-call(s32[24]{0:T(128)S(1)} %dynamic-slice_bitcast_fusion.idx_ref, bf16[128,4096]{1,0:T(8,128)(2,1)S(1)} %bitcast.41, bf16[128,4096]{1,0:T(8,128)(2,1)S(1)} %bitcast.43, f32[32,128]{1,0:T(8,128)S(1)} %get-tuple-element.32.lse_ref, ...), custom_call_target="tpu_custom_call" | custom-call | flops 1610612736 | bytes 10485760 | tf_op jit(solution)/shard_map/scores_dq_dk/pallas_call | solution.py:279
  80.8 2.1 %collective-permute-done.29 = bf16[256,512]{1,0:T(8,128)(2,1)S(1)} collective-permute-done((bf16[256,512]{1,0:T(8,128)(2,1)S(1)}, bf16[256,512]{1,0:T(8,128)(2,1)S(1)}, u32[]{:S(2)}, u32[]{:S(2)}) %collective-permute-start.29) | collective-permute-done | bytes 262176 | tf_op jit(solution)/shard_map/ppermute | solution.py:457
  83.0 1.6 %collective-permute-start.24 = (bf16[256,512]{1,0:T(8,128)(2,1)S(1)}, bf16[256,512]{1,0:T(8,128)(2,1)S(1)}, u32[]{:S(2)}, u32[]{:S(2)}) collective-permute-start(bf16[256,512]{1,0:T(8,128)(2,1)S(1)} %get-tuple-element.52), channel_id=1, source_target_pairs={{0,4},{8,12},{16,20},{24,28},{4,0},{12,8},{20,16},{28,24},{1,5},{9... | collective-permute-start | bytes 786440 | tf_op jit(solution)/shard_map/ppermute | solution.py:457
  86.1 2.2 %collective-permute-start.28 = (bf16[256,512]{1,0:T(8,128)(2,1)S(1)}, bf16[256,512]{1,0:T(8,128)(2,1)S(1)}, u32[]{:S(2)}, u32[]{:S(2)}) collective-permute-start(bf16[256,512]{1,0:T(8,128)(2,1)S(1)} %fusion.2), channel_id=1, source_target_pairs={{0,16},{4,20},{16,24},{20,28},{24,8},{28,12},{8,0},{12,4},{1,17},{... | collective-permute-start | bytes 786440 | tf_op jit(solution)/shard_map/ppermute | solution.py:454
  88.4 7.4 %collective-permute-done.23.rest_3_ = bf16[128,2048]{1,0:T(8,128)(2,1)S(1)} collective-permute-done((bf16[128,2048]{1,0:T(8,128)(2,1)S(1)}, bf16[128,2048]{1,0:T(8,128)(2,1)S(1)}, u32[]{:S(2)}, u32[]{:S(2)}) %collective-permute-start.23) | collective-permute-done | bytes 524320 | tf_op jit(solution)/shard_map/ppermute | solution.py:436
  95.7 2.5 %join_columns.1 = bf16[128,8192]{1,0:T(8,128)(2,1)} custom-call(s32[24]{0:T(128)S(1)} %dynamic-slice_bitcast_fusion.idx_ref, bf16[128,2048]{1,0:T(8,128)(2,1)S(1)} %get-tuple-element.47.rest_0_, bf16[128,2048]{1,0:T(8,128)(2,1)S(1)} %collective-permute-done.21.rest_1_, bf16[128,2048]{1,0:T(8,128)(2,1)S(1)} %collective-permute-done.22.rest_2_, ...), custom_call_target="tpu_custom_call" | custom-call | bytes 4194304 | tf_op jit(solution)/shard_map/join_columns/pallas_call | solution.py:105
  98.4 1.5 %collective-permute-start.17 = (bf16[128,512]{1,0:T(8,128)(2,1)S(1)}, bf16[128,512]{1,0:T(8,128)(2,1)S(1)}, u32[]{:S(2)}, u32[]{:S(2)}) collective-permute-start(bf16[128,512]{1,0:T(8,128)(2,1)S(1)} %fusion.9), channel_id=1, source_target_pairs={{0,2},{1,3},{2,0},{3,1},{4,6},{5,7},{6,4},{7,5},{8,10},{9,11},{10,... | collective-permute-start | bytes 393224 | tf_op jit(solution)/shard_map/ppermute | solution.py:436
  100.8 3.6 %collective-permute-done.17 = bf16[128,512]{1,0:T(8,128)(2,1)S(1)} collective-permute-done((bf16[128,512]{1,0:T(8,128)(2,1)S(1)}, bf16[128,512]{1,0:T(8,128)(2,1)S(1)}, u32[]{:S(2)}, u32[]{:S(2)}) %collective-permute-start.17) | collective-permute-done | bytes 131104 | tf_op jit(solution)/shard_map/ppermute | solution.py:436
  (62 shorter events, 12.3 us)
Async XLA Ops:
  0.6 19.1 %copy-start = (bf16[256,512]{1,0:T(8,128)(2,1)S(1)}, bf16[256,512]{1,0:T(8,128)(2,1)}, u32[]{:S(2)}) copy-start(bf16[256,512]{1,0:T(8,128)(2,1)} %rest_0_.1) | copy-start | bytes 786436
  1.6 6.9 %collective-permute-start = (bf16[144,512]{1,0:T(8,128)(2,1)S(1)}, bf16[144,512]{1,0:T(8,128)(2,1)S(1)}, u32[]{:S(2)}, u32[]{:S(2)}) collective-permute-start(bf16[144,512]{1,0:T(8,128)(2,1)S(1)} %key_block.1.rest_0_), channel_id=1, source_target_pairs={{0,2},{1,3},{2,0},{3,1},{4,6},{5,7},{6,4},{7,5},{8,10},{9,11},{10,... | collective-permute-start | bytes 442376 | tf_op jit(solution)/shard_map/ppermute | solution.py:436
  4.6 7.4 %collective-permute-start.1 = (bf16[144,512]{1,0:T(8,128)(2,1)S(1)}, bf16[144,512]{1,0:T(8,128)(2,1)S(1)}, u32[]{:S(2)}, u32[]{:S(2)}) collective-permute-start(bf16[144,512]{1,0:T(8,128)(2,1)S(1)} %key_block.1.rest_0_), channel_id=1, source_target_pairs={{0,1},{1,0},{2,3},{3,2},{4,5},{5,4},{6,7},{7,6},{8,9},{9,8},{10,11... | collective-permute-start | bytes 442376 | tf_op jit(solution)/shard_map/ppermute | solution.py:436
  8.5 3.5 %collective-permute-start.2 = (bf16[144,512]{1,0:T(8,128)(2,1)S(1)}, bf16[144,512]{1,0:T(8,128)(2,1)S(1)}, u32[]{:S(2)}, u32[]{:S(2)}) collective-permute-start(bf16[144,512]{1,0:T(8,128)(2,1)S(1)} %collective-permute-done.rest_1_), channel_id=1, source_target_pairs={{0,1},{1,0},{2,3},{3,2},{4,5},{5,4},{6,7},{7,6},{8,9},{9,8},{10,11... | collective-permute-start | bytes 442376 | tf_op jit(solution)/shard_map/ppermute | solution.py:436
  8.5 12.8 %collective-permute-start.7 = (bf16[256,512]{1,0:T(8,128)(2,1)}, bf16[256,512]{1,0:T(8,128)(2,1)S(1)}, u32[]{:S(2)}, u32[]{:S(2)}) collective-permute-start(bf16[256,512]{1,0:T(8,128)(2,1)} %rest_0_.1), channel_id=1, source_target_pairs={{0,16},{4,20},{16,24},{20,28},{24,8},{28,12},{8,0},{12,4},{1,17},{... | collective-permute-start | bytes 786440 | tf_op jit(solution)/shard_map/ppermute | solution.py:454
  19.5 17.0 %collective-permute-start.18 = (f32[2,128,512]{2,1,0:T(8,128)S(1)}, f32[2,128,512]{2,1,0:T(8,128)S(1)}, u32[]{:S(2)}, u32[]{:S(2)}) collective-permute-start(f32[2,128,512]{2,1,0:T(8,128)S(1)} %get-tuple-element.46), channel_id=1, source_target_pairs={{0,1},{1,0},{2,3},{3,2},{4,5},{5,4},{6,7},{7,6},{8,9},{9,8},{10,11... | collective-permute-start | bytes 1572872 | tf_op jit(solution)/shard_map/ppermute | solution.py:436
  19.8 10.1 %collective-permute-start.11 = (bf16[256,512]{1,0:T(8,128)(2,1)S(1)}, bf16[256,512]{1,0:T(8,128)(2,1)S(1)}, u32[]{:S(2)}, u32[]{:S(2)}) collective-permute-start(bf16[256,512]{1,0:T(8,128)(2,1)S(1)} %copy-done), channel_id=1, source_target_pairs={{16,0},{20,4},{24,16},{28,20},{8,24},{12,28},{0,8},{4,12},{17,1},{... | collective-permute-start | bytes 786440 | tf_op jit(solution)/shard_map/ppermute | solution.py:454
  19.8 11.5 %collective-permute-start.6 = (bf16[256,512]{1,0:T(8,128)(2,1)S(1)}, bf16[256,512]{1,0:T(8,128)(2,1)S(1)}, u32[]{:S(2)}, u32[]{:S(2)}) collective-permute-start(bf16[256,512]{1,0:T(8,128)(2,1)S(1)} %copy-done), channel_id=1, source_target_pairs={{0,4},{8,12},{16,20},{24,28},{4,0},{12,8},{20,16},{28,24},{1,5},{9... | collective-permute-start | bytes 786440 | tf_op jit(solution)/shard_map/ppermute | solution.py:457
  21.3 13.5 %collective-permute-start.9 = (bf16[256,512]{1,0:T(8,128)(2,1)S(1)}, bf16[256,512]{1,0:T(8,128)(2,1)S(1)}, u32[]{:S(2)}, u32[]{:S(2)}) collective-permute-start(bf16[256,512]{1,0:T(8,128)(2,1)S(1)} %collective-permute-done.7.rest_6_.rest_2_), channel_id=1, source_target_pairs={{0,16},{4,20},{16,24},{20,28},{24,8},{28,12},{8,0},{12,4},{1,17},{... | collective-permute-start | bytes 786440 | tf_op jit(solution)/shard_map/ppermute | solution.py:454
  24.2 11.7 %collective-permute-start.8 = (bf16[256,512]{1,0:T(8,128)(2,1)S(1)}, bf16[256,512]{1,0:T(8,128)(2,1)S(1)}, u32[]{:S(2)}, u32[]{:S(2)}) collective-permute-start(bf16[256,512]{1,0:T(8,128)(2,1)S(1)} %collective-permute-done.7.rest_6_.rest_2_), channel_id=1, source_target_pairs={{0,4},{8,12},{16,20},{24,28},{4,0},{12,8},{20,16},{28,24},{1,5},{9... | collective-permute-start | bytes 786440 | tf_op jit(solution)/shard_map/ppermute | solution.py:457
  29.8 15.8 %collective-permute-start.3 = (bf16[128,2048]{1,0:T(8,128)(2,1)S(1)}, bf16[128,2048]{1,0:T(8,128)(2,1)S(1)}, u32[]{:S(2)}, u32[]{:S(2)}) collective-permute-start(bf16[128,2048]{1,0:T(8,128)(2,1)S(1)} %get-tuple-element.35), channel_id=1, source_target_pairs={{0,2},{1,3},{2,0},{3,1},{4,6},{5,7},{6,4},{7,5},{8,10},{9,11},{10,... | collective-permute-start | bytes 1572872 | tf_op jit(solution)/shard_map/ppermute | solution.py:436
  31.3 14.3 %collective-permute-start.4 = (bf16[128,2048]{1,0:T(8,128)(2,1)S(1)}, bf16[128,2048]{1,0:T(8,128)(2,1)S(1)}, u32[]{:S(2)}, u32[]{:S(2)}) collective-permute-start(bf16[128,2048]{1,0:T(8,128)(2,1)S(1)} %get-tuple-element.37), channel_id=1, source_target_pairs={{0,1},{1,0},{2,3},{3,2},{4,5},{5,4},{6,7},{7,6},{8,9},{9,8},{10,11... | collective-permute-start | bytes 1572872 | tf_op jit(solution)/shard_map/ppermute | solution.py:436
  34.8 20.1 %collective-permute-start.5 = (bf16[128,2048]{1,0:T(8,128)(2,1)S(1)}, bf16[128,2048]{1,0:T(8,128)(2,1)S(1)}, u32[]{:S(2)}, u32[]{:S(2)}) collective-permute-start(bf16[128,2048]{1,0:T(8,128)(2,1)S(1)} %get-tuple-element.39), channel_id=1, source_target_pairs={{0,3},{1,2},{2,1},{3,0},{4,7},{5,6},{6,5},{7,4},{8,11},{9,10},{10,... | collective-permute-start | bytes 1572872 | tf_op jit(solution)/shard_map/ppermute | solution.py:436
  35.9 9.2 %collective-permute-start.12 = (bf16[256,512]{1,0:T(8,128)(2,1)S(1)}, bf16[256,512]{1,0:T(8,128)(2,1)S(1)}, u32[]{:S(2)}, u32[]{:S(2)}) collective-permute-start(bf16[256,512]{1,0:T(8,128)(2,1)S(1)} %collective-permute-done.11.rest_10_.rest_6_), channel_id=1, source_target_pairs={{0,4},{8,12},{16,20},{24,28},{4,0},{12,8},{20,16},{28,24},{1,5},{9... | collective-permute-start | bytes 786440 | tf_op jit(solution)/shard_map/ppermute | solution.py:457
  36.5 18.3 %collective-permute-start.10 = (bf16[256,512]{1,0:T(8,128)(2,1)S(1)}, bf16[256,512]{1,0:T(8,128)(2,1)S(1)}, u32[]{:S(2)}, u32[]{:S(2)}) collective-permute-start(bf16[256,512]{1,0:T(8,128)(2,1)S(1)} %collective-permute-done.9.rest_8_.rest_4_), channel_id=1, source_target_pairs={{0,4},{8,12},{16,20},{24,28},{4,0},{12,8},{20,16},{28,24},{1,5},{9... | collective-permute-start | bytes 786440 | tf_op jit(solution)/shard_map/ppermute | solution.py:457
  45.1 14.2 %collective-permute-start.19 = (bf16[2,128,512]{2,1,0:T(8,128)(2,1)S(1)}, bf16[2,128,512]{2,1,0:T(8,128)(2,1)S(1)}, u32[]{:S(2)}, u32[]{:S(2)}) collective-permute-start(bf16[2,128,512]{2,1,0:T(8,128)(2,1)S(1)} %get-tuple-element.60), channel_id=1, source_target_pairs={{0,2},{1,3},{2,0},{3,1},{4,6},{5,7},{6,4},{7,5},{8,10},{9,11},{10,... | collective-permute-start | bytes 786440 | tf_op jit(solution)/shard_map/ppermute | solution.py:436
  56.8 2.7 %collective-permute-start.13 = (f32[2,128,512]{2,1,0:T(8,128)S(1)}, f32[2,128,512]{2,1,0:T(8,128)S(1)}, u32[]{:S(2)}, u32[]{:S(2)}) collective-permute-start(f32[2,128,512]{2,1,0:T(8,128)S(1)} %get-tuple-element.41), channel_id=1, source_target_pairs={{0,1},{1,0},{2,3},{3,2},{4,5},{5,4},{6,7},{7,6},{8,9},{9,8},{10,11... | collective-permute-start | bytes 1572872 | tf_op jit(solution)/shard_map/ppermute | solution.py:436
  59.4 1.7 %collective-permute-start.20 = (bf16[2,128,512]{2,1,0:T(8,128)(2,1)S(1)}, bf16[2,128,512]{2,1,0:T(8,128)(2,1)S(1)}, u32[]{:S(2)}, u32[]{:S(2)}) collective-permute-start(bf16[2,128,512]{2,1,0:T(8,128)(2,1)S(1)} %add_convert_fusion.g0.rest_4_), channel_id=1, source_target_pairs={{0,1},{1,0},{2,3},{3,2},{4,5},{5,4},{6,7},{7,6},{8,9},{9,8},{10,11... | collective-permute-start | bytes 786440 | tf_op jit(solution)/shard_map/ppermute | solution.py:436
  59.6 8.8 %collective-permute-start.14 = (bf16[2,128,512]{2,1,0:T(8,128)(2,1)S(1)}, bf16[2,128,512]{2,1,0:T(8,128)(2,1)S(1)}, u32[]{:S(2)}, u32[]{:S(2)}) collective-permute-start(bf16[2,128,512]{2,1,0:T(8,128)(2,1)S(1)} %get-tuple-element.62), channel_id=1, source_target_pairs={{0,2},{1,3},{2,0},{3,1},{4,6},{5,7},{6,4},{7,5},{8,10},{9,11},{10,... | collective-permute-start | bytes 786440 | tf_op jit(solution)/shard_map/ppermute | solution.py:436
  63.2 9.2 %collective-permute-start.25 = (bf16[256,512]{1,0:T(8,128)(2,1)S(1)}, bf16[256,512]{1,0:T(8,128)(2,1)S(1)}, u32[]{:S(2)}, u32[]{:S(2)}) collective-permute-start(bf16[256,512]{1,0:T(8,128)(2,1)S(1)} %get-tuple-element.54), channel_id=1, source_target_pairs={{0,4},{8,12},{16,20},{24,28},{4,0},{12,8},{20,16},{28,24},{1,5},{9... | collective-permute-start | bytes 786440 | tf_op jit(solution)/shard_map/ppermute | solution.py:457
  64.8 14.8 %collective-permute-start.27 = (bf16[256,512]{1,0:T(8,128)(2,1)S(1)}, bf16[256,512]{1,0:T(8,128)(2,1)S(1)}, u32[]{:S(2)}, u32[]{:S(2)}) collective-permute-start(bf16[256,512]{1,0:T(8,128)(2,1)S(1)} %get-tuple-element.56), channel_id=1, source_target_pairs={{0,4},{8,12},{16,20},{24,28},{4,0},{12,8},{20,16},{28,24},{1,5},{9... | collective-permute-start | bytes 786440 | tf_op jit(solution)/shard_map/ppermute | solution.py:457
  65.3 17.6 %collective-permute-start.29 = (bf16[256,512]{1,0:T(8,128)(2,1)S(1)}, bf16[256,512]{1,0:T(8,128)(2,1)S(1)}, u32[]{:S(2)}, u32[]{:S(2)}) collective-permute-start(bf16[256,512]{1,0:T(8,128)(2,1)S(1)} %get-tuple-element.58), channel_id=1, source_target_pairs={{0,4},{8,12},{16,20},{24,28},{4,0},{12,8},{20,16},{28,24},{1,5},{9... | collective-permute-start | bytes 786440 | tf_op jit(solution)/shard_map/ppermute | solution.py:457
  68.5 4.1 %collective-permute-start.15 = (bf16[2,128,512]{2,1,0:T(8,128)(2,1)S(1)}, bf16[2,128,512]{2,1,0:T(8,128)(2,1)S(1)}, u32[]{:S(2)}, u32[]{:S(2)}) collective-permute-start(bf16[2,128,512]{2,1,0:T(8,128)(2,1)S(1)} %add_convert_fusion.1.v0_ref), channel_id=1, source_target_pairs={{0,1},{1,0},{2,3},{3,2},{4,5},{5,4},{6,7},{7,6},{8,9},{9,8},{10,11... | collective-permute-start | bytes 786440 | tf_op jit(solution)/shard_map/ppermute | solution.py:436
  70.6 14.9 %collective-permute-start.21 = (bf16[128,2048]{1,0:T(8,128)(2,1)S(1)}, bf16[128,2048]{1,0:T(8,128)(2,1)S(1)}, u32[]{:S(2)}, u32[]{:S(2)}) collective-permute-start(bf16[128,2048]{1,0:T(8,128)(2,1)S(1)} %get-tuple-element.48), channel_id=1, source_target_pairs={{0,2},{1,3},{2,0},{3,1},{4,6},{5,7},{6,4},{7,5},{8,10},{9,11},{10,... | collective-permute-start | bytes 1572872 | tf_op jit(solution)/shard_map/ppermute | solution.py:436
  72.5 13.6 %collective-permute-start.22 = (bf16[128,2048]{1,0:T(8,128)(2,1)S(1)}, bf16[128,2048]{1,0:T(8,128)(2,1)S(1)}, u32[]{:S(2)}, u32[]{:S(2)}) collective-permute-start(bf16[128,2048]{1,0:T(8,128)(2,1)S(1)} %get-tuple-element.49), channel_id=1, source_target_pairs={{0,1},{1,0},{2,3},{3,2},{4,5},{5,4},{6,7},{7,6},{8,9},{9,8},{10,11... | collective-permute-start | bytes 1572872 | tf_op jit(solution)/shard_map/ppermute | solution.py:436
  72.6 10.5 %collective-permute-start.26 = (bf16[256,512]{1,0:T(8,128)(2,1)S(1)}, bf16[256,512]{1,0:T(8,128)(2,1)S(1)}, u32[]{:S(2)}, u32[]{:S(2)}) collective-permute-start(bf16[256,512]{1,0:T(8,128)(2,1)S(1)} %fusion.3), channel_id=1, source_target_pairs={{0,16},{4,20},{16,24},{20,28},{24,8},{28,12},{8,0},{12,4},{1,17},{... | collective-permute-start | bytes 786440 | tf_op jit(solution)/shard_map/ppermute | solution.py:454
  79.6 16.1 %collective-permute-start.23 = (bf16[128,2048]{1,0:T(8,128)(2,1)S(1)}, bf16[128,2048]{1,0:T(8,128)(2,1)S(1)}, u32[]{:S(2)}, u32[]{:S(2)}) collective-permute-start(bf16[128,2048]{1,0:T(8,128)(2,1)S(1)} %get-tuple-element.51), channel_id=1, source_target_pairs={{0,3},{1,2},{2,1},{3,0},{4,7},{5,6},{6,5},{7,4},{8,11},{9,10},{10,... | collective-permute-start | bytes 1572872 | tf_op jit(solution)/shard_map/ppermute | solution.py:436
  82.9 15.3 %collective-permute-start.16 = (f32[2,128,512]{2,1,0:T(8,128)S(1)}, f32[2,128,512]{2,1,0:T(8,128)S(1)}, u32[]{:S(2)}, u32[]{:S(2)}) collective-permute-start(f32[2,128,512]{2,1,0:T(8,128)S(1)} %get-tuple-element.44), channel_id=1, source_target_pairs={{0,1},{1,0},{2,3},{3,2},{4,5},{5,4},{6,7},{7,6},{8,9},{9,8},{10,11... | collective-permute-start | bytes 1572872 | tf_op jit(solution)/shard_map/ppermute | solution.py:436
  83.0 16.9 %collective-permute-start.24 = (bf16[256,512]{1,0:T(8,128)(2,1)S(1)}, bf16[256,512]{1,0:T(8,128)(2,1)S(1)}, u32[]{:S(2)}, u32[]{:S(2)}) collective-permute-start(bf16[256,512]{1,0:T(8,128)(2,1)S(1)} %get-tuple-element.52), channel_id=1, source_target_pairs={{0,4},{8,12},{16,20},{24,28},{4,0},{12,8},{20,16},{28,24},{1,5},{9... | collective-permute-start | bytes 786440 | tf_op jit(solution)/shard_map/ppermute | solution.py:457
  85.4 14.5 %collective-permute-start.30 = (bf16[256,512]{1,0:T(8,128)(2,1)S(1)}, bf16[256,512]{1,0:T(8,128)(2,1)S(1)}, u32[]{:S(2)}, u32[]{:S(2)}) collective-permute-start(bf16[256,512]{1,0:T(8,128)(2,1)S(1)} %fusion), channel_id=1, source_target_pairs={{16,0},{20,4},{24,16},{28,20},{8,24},{12,28},{0,8},{4,12},{17,1},{... | collective-permute-start | bytes 786440 | tf_op jit(solution)/shard_map/ppermute | solution.py:454
  86.1 13.8 %collective-permute-start.28 = (bf16[256,512]{1,0:T(8,128)(2,1)S(1)}, bf16[256,512]{1,0:T(8,128)(2,1)S(1)}, u32[]{:S(2)}, u32[]{:S(2)}) collective-permute-start(bf16[256,512]{1,0:T(8,128)(2,1)S(1)} %fusion.2), channel_id=1, source_target_pairs={{0,16},{4,20},{16,24},{20,28},{24,8},{28,12},{8,0},{12,4},{1,17},{... | collective-permute-start | bytes 786440 | tf_op jit(solution)/shard_map/ppermute | solution.py:454
  98.4 6.1 %collective-permute-start.17 = (bf16[128,512]{1,0:T(8,128)(2,1)S(1)}, bf16[128,512]{1,0:T(8,128)(2,1)S(1)}, u32[]{:S(2)}, u32[]{:S(2)}) collective-permute-start(bf16[128,512]{1,0:T(8,128)(2,1)S(1)} %fusion.9), channel_id=1, source_target_pairs={{0,2},{1,3},{2,0},{3,1},{4,6},{5,7},{6,4},{7,5},{8,10},{9,11},{10,... | collective-permute-start | bytes 393224 | tf_op jit(solution)/shard_map/ppermute | solution.py:436
  (4 other events, 12.0 us)
where the time goes:
time: 105 us
  waiting for transfers between devices  43.8 us (42%)
  starting transfers between devices  32 us (30%)
  Pallas kernels  23 us (22%)
  local copies, waits for them, and re-layouts  3.21 us (3%)
  other arithmetic  2.27 us (2%)
    ppermute x17, waiting for transfers between devices, send_sp(): return lax.ppermute(v, 'sp', sp_perm(dx % nx, dc))  27.9 us
    ppermute x17, starting transfers between devices, send_sp(): return lax.ppermute(v, 'sp', sp_perm(dx % nx, dc))  13.3 us
    ppermute x8, waiting for transfers between devices, send_y(): return lax.ppermute(v, 'dp', y_next)  9.54 us
    ppermute x6, starting transfers between devices, send_z(): return lax.ppermute(v, 'dp', z_next if forward else z_back)  9.38 us
    ppermute x8, starting transfers between devices, send_y(): return lax.ppermute(v, 'dp', y_next)  9.26 us
    ppermute x6, waiting for transfers between devices, send_z(): return lax.ppermute(v, 'dp', z_next if forward else z_back)  6.4 us
    pallas_call x1, Pallas kernels, scores_call(): pl.pallas_call(functools.partial(scores_kernel, sp, tok, win, group, pair...  6.38 us
    pallas_call x1, Pallas kernels, probs_call(): pl.pallas_call(functools.partial(probs_kernel, sp, tok, win, group, pair)...  4.97 us
  transfers between devices with their start and end apart: 31, of which 12 were waited for; matrix products, arithmetic and copies ran while one was open for 2% of the time, Pallas kernels for 21%

commit v1 on v0

--- a/solution.py
+++ b/solution.py
@@ -154,6 +154,8 @@
     at = pl.ds(pl.multiple_of(head * HD, HD), HD)
     for r in range(sp):
         key_hold[rows_at(idx_ref[r], tok), :] = kd_refs[r][0:tok, at]
+    if bias is None:
+        return first, at
 
     @pl.when(head == 0)
     def _():
@@ -187,8 +189,9 @@
 
 
 def probs_kernel(sp, tok, win, group, pair, idx_ref, q_ref, g_ref, *rest):
-    kds, (keep, send, lse_ref) = rest[:sp], rest[sp : sp + 3]
-    key_hold, doc_hold, bias, q_st, g_st, p_st, acc = rest[sp + 3 :]
+    kds, (keep, send, p_ref) = rest[:sp], rest[sp : sp + 3]
+    key_hold, doc_hold, bias, q_st, g_st, acc = rest[sp + 3 :]
+    p_st = p_ref.at[pl.program_id(0)]
     first, cols = fill_keys(sp, tok, win, pair, idx_ref, kds, key_hold, doc_hold, bias)
     factor = F32(HD**-0.5 * math.log2(math.e))
     stack_heads(q_ref, q_st, tok, group)
@@ -201,9 +204,6 @@
         e = jnp.exp2(s - top)
         total = jnp.sum(e, axis=0, keepdims=True)
         p_st[:, at] = (e * (1.0 / total)).astype(BF)
-        lse = top + jnp.log2(total)
-        for i in range(pair):
-            lse_ref[h + i : h + i + 1, :] = lse[:, i * tok : (i + 1) * tok]
     emit_rel(
         acc, first, dot(p_st[...], g_st[...], NN), sp, tok, win, cols, idx_ref, keep, send
     )
@@ -215,19 +215,18 @@
     wide = pl.BlockSpec((tok, group * HD), lambda c, _: (0, c))
     return pl.pallas_call(
         functools.partial(probs_kernel, sp, tok, win, group, pair),
-        out_shape=[part, part, jax.ShapeDtypeStruct((kvh * group, tok), F32)],
+        out_shape=[part, part, jax.ShapeDtypeStruct((kvh, win * tok, group * tok), BF)],
         grid_spec=pltpu.PrefetchScalarGridSpec(
             num_scalar_prefetch=1,
             grid=(kvh,),
             in_specs=[wide, wide] + [VM] * sp,
-            out_specs=[VM, VM, pl.BlockSpec((group, tok), lambda c, _: (c, 0))],
+            out_specs=[VM, VM, VM],
             scratch_shapes=[
                 pltpu.VMEM((seq, HD), BF),
                 pltpu.VMEM((sp, 16, tok), F32),
                 pltpu.VMEM((win * tok, pair * tok), F32),
                 pltpu.VMEM((group * tok, HD), BF),
                 pltpu.VMEM((group * tok, HD), BF),
-                pltpu.VMEM((win * tok, group * tok), BF),
                 pltpu.VMEM((seq, HD), F32),
             ],
         ),
@@ -241,38 +240,34 @@
     )(idx, q, g, *kds)
 
 
-def scores_kernel(sp, tok, win, group, pair, idx_ref, q_ref, g_ref, lse_ref, v0_ref, v1_ref, *rest):
+def scores_kernel(sp, tok, win, group, pair, idx_ref, q_ref, g_ref, p_ref, v0_ref, v1_ref, *rest):
     nx = sp // 2
     kds, (dq_ref, keep, send) = rest[:sp], rest[sp : sp + 3]
-    key_hold, doc_hold, bias, val_hold, q_st, g_st, ds_st, acc = rest[sp + 3 :]
-    first, cols = fill_keys(sp, tok, win, pair, idx_ref, kds, key_hold, doc_hold, bias)
+    key_hold, val_hold, q_st, g_st, ds_st, acc = rest[sp + 3 :]
+    first, cols = fill_keys(sp, tok, win, pair, idx_ref, kds, key_hold, None, None)
     for dx in range(nx):
         val_hold[rows_at(idx_ref[dx], tok), :] = v0_ref[dx, :, cols]
         val_hold[rows_at(idx_ref[nx + dx], tok), :] = v1_ref[dx, :, cols]
-    scale = HD**-0.5
-    factor = F32(scale * math.log2(math.e))
+    scale = F32(HD**-0.5)
     stack_heads(q_ref, q_st, tok, group)
     stack_heads(g_ref, g_st, tok, group)
     window = pl.ds(pl.multiple_of(first * tok, tok), win * tok)
     keys, vals = key_hold[window, :], val_hold[window, :]
+    p_st = p_ref.at[pl.program_id(0)]
     for h in range(0, group, pair):
         at = slice(h * tok, (h + pair) * tok)
-        lse = jnp.concatenate([lse_ref[h + i : h + i + 1, :] for i in range(pair)], axis=1)
-        shift = lse - F32(math.log2(scale))
-        s = dot(keys, q_st[at, :], NT) * factor + bias[...]
-        scaled = jnp.exp2(s - shift)
         dp = dot(vals, g_st[at, :], NT)
-        delta = jnp.sum(scaled * dp, axis=0, keepdims=True) * F32(1.0 / scale)
-        ds_st[:, at] = (scaled * (dp - delta)).astype(BF)
-    dq = dot(ds_st[...], keys, TN)
+        probs = p_st[:, at].astype(F32)
+        delta = jnp.sum(probs * dp, axis=0, keepdims=True)
+        ds_st[:, at] = (probs * (dp - delta)).astype(BF)
+    dq = dot(ds_st[...], keys, TN) * scale
     for h in range(group):
         dq_ref[:, h * HD : (h + 1) * HD] = dq[h * tok : (h + 1) * tok, :].astype(BF)
-    emit_rel(
-        acc, first, dot(ds_st[...], q_st[...], NN), sp, tok, win, cols, idx_ref, keep, send
-    )
-
-
-def scores_call(idx, q, g, lse, v0, v1, kds, sp, tok, win, kvh, group):
+    dk = dot(ds_st[...], q_st[...], NN) * scale
+    emit_rel(acc, first, dk, sp, tok, win, cols, idx_ref, keep, send)
+
+
+def scores_call(idx, q, g, p, v0, v1, kds, sp, tok, win, kvh, group):
     nx, seq, pair = sp // 2, sp * tok, 2
     part = jax.ShapeDtypeStruct((nx, tok, kvh * HD), F32)
     wide = pl.BlockSpec((tok, group * HD), lambda c, _: (0, c))
@@ -282,13 +277,10 @@
         grid_spec=pltpu.PrefetchScalarGridSpec(
             num_scalar_prefetch=1,
             grid=(kvh,),
-            in_specs=[wide, wide, pl.BlockSpec((group, tok), lambda c, _: (c, 0)), VM, VM]
-            + [VM] * sp,
+            in_specs=[wide, wide] + [VM] * (3 + sp),
             out_specs=[wide, VM, VM],
             scratch_shapes=[
                 pltpu.VMEM((seq, HD), BF),
-                pltpu.VMEM((sp, 16, tok), F32),
-                pltpu.VMEM((win * tok, pair * tok), F32),
                 pltpu.VMEM((seq, HD), BF),
                 pltpu.VMEM((group * tok, HD), BF),
                 pltpu.VMEM((group * tok, HD), BF),
@@ -298,12 +290,12 @@
         ),
         compiler_params=grant(24),
         cost_estimate=pl.CostEstimate(
-            flops=8 * tok * win * tok * kvh * group * HD,
+            flops=6 * tok * win * tok * kvh * group * HD,
             bytes_accessed=10 * MIB,
-            transcendentals=tok * win * tok * kvh * group,
+            transcendentals=0,
         ),
         name="scores_dq_dk",
-    )(idx, q, g, lse, v0, v1, *kds)
+    )(idx, q, g, p, v0, v1, *kds)
 
 
 def values_kernel(sp, dp, tok, width, base, idx_ref, *rest):
@@ -500,7 +492,7 @@
     pieces = split_columns(idx, at_fwd, layer_input[0], sp, dp, width)
     ready = [pieces[0]] + [after(v, near[-1]) for v in pieces[1:]]
 
-    dv_keep, dv_send, lse = probs_call(idx, q, g, kds, sp, tok, win, kvh, group)
+    dv_keep, dv_send, probs = probs_call(idx, q, g, kds, sp, tok, win, kvh, group)
 
     def reduce_core(keep, send):
         return keep + send_sp(send, 0, 1)
@@ -515,12 +507,15 @@
         mine = total.astype(BF)
         return mine, send_sp(mine, 0, 1), got
 
-    vg0, vg1, _ = reduce_all(dv_keep, dv_send)
+    vg0, vg1, vg_got = reduce_all(dv_keep, dv_send)
 
     xs = [pieces[0]]
     for r in range(1, sp):
         dx, dc = r % nx, r // nx
-        xs.append(send_sp(ready[r], dx, dc))
+        if dx and dc:
+            xs.append(send_sp(after(ready[r], vg_got), dx, dc))
+        else:
+            xs.append(send_sp(ready[r], dx, dc))
 
     parts = igrad_call(idx, at_gather, vg0, vg1, rows, sp, dp, tok, width)
 
@@ -542,7 +537,7 @@
 
     v_keep, v_send = values_call(idx, at_gather, xs, rows, sp, dp, tok, width)
     v0, v1, v_got = reduce_all(v_keep, v_send)
-    dq, dk_keep, dk_send = scores_call(idx, q, g, lse, v0, v1, kds, sp, tok, win, kvh, group)
+    dq, dk_keep, dk_send = scores_call(idx, q, g, probs, v0, v1, kds, sp, tok, win, kvh, group)
     dk = reduce_core(dk_keep, dk_send)
     key_sum = dk[0]
     for k in range(1, nx):

time: 105 us -> 111 us (1.057)
  the two profiles are of different devices: /device:TPU:0 before, /device:TPU:1 now
where the time goes in v1:
time: 111 us
  waiting for transfers between devices  44.8 us (40%)
  starting transfers between devices  36.7 us (33%)
  Pallas kernels  23.4 us (21%)
  local copies, waits for them, and re-layouts  3.21 us (3%)
  other arithmetic  2.29 us (2%)
    ppermute x17, waiting for transfers between devices, send_sp(): return lax.ppermute(v, 'sp', sp_perm(dx % nx, dc))  26.7 us
    ppermute x17, starting transfers between devices, send_sp(): return lax.ppermute(v, 'sp', sp_perm(dx % nx, dc))  17.4 us
    ppermute x8, waiting for transfers between devices, send_y(): return lax.ppermute(v, 'dp', y_next)  10.4 us
    ppermute x8, starting transfers between devices, send_y(): return lax.ppermute(v, 'dp', y_next)  10.2 us
    ppermute x6, starting transfers between devices, send_z(): return lax.ppermute(v, 'dp', z_next if forward else z_back)  8.99 us
    ppermute x6, waiting for transfers between devices, send_z(): return lax.ppermute(v, 'dp', z_next if forward else z_back)  7.72 us
    pallas_call x1, Pallas kernels, scores_call(): pl.pallas_call(functools.partial(scores_kernel, sp, tok, win, group, pair...  6.06 us
    pallas_call x1, Pallas kernels, probs_call(): pl.pallas_call(functools.partial(probs_kernel, sp, tok, win, group, pair)...  5.64 us
  transfers between devices with their start and end apart: 31, of which 15 were waited for; matrix products, arithmetic and copies ran while one was open for 2% of the time, Pallas kernels for 13%

profile of v1, /device:TPU:1, one launch (start us, length us, event | category | flops | bytes accessed | tf_op | source)
XLA Modules:
  0.0 111.2 jit_solution(12723484279597033209)
XLA Ops:
  1.6 2.1 %collective-permute-start = (bf16[144,512]{1,0:T(8,128)(2,1)S(1)}, bf16[144,512]{1,0:T(8,128)(2,1)S(1)}, u32[]{:S(2)}, u32[]{:S(2)}) collective-permute-start(bf16[144,512]{1,0:T(8,128)(2,1)S(1)} %key_block.1.rest_0_), channel_id=1, source_target_pairs={{0,2},{1,3},{2,0},{3,1},{4,6},{5,7},{6,4},{7,5},{8,10},{9,11},{10,... | collective-permute-start | bytes 442376 | tf_op jit(solution)/shard_map/ppermute | solution.py:428
  4.7 2.6 %collective-permute-done.rest_1_ = bf16[144,512]{1,0:T(8,128)(2,1)S(1)} collective-permute-done((bf16[144,512]{1,0:T(8,128)(2,1)S(1)}, bf16[144,512]{1,0:T(8,128)(2,1)S(1)}, u32[]{:S(2)}, u32[]{:S(2)}) %collective-permute-start) | collective-permute-done | bytes 147488 | tf_op jit(solution)/shard_map/ppermute | solution.py:428
  7.3 1.3 %collective-permute-start.2 = (bf16[144,512]{1,0:T(8,128)(2,1)S(1)}, bf16[144,512]{1,0:T(8,128)(2,1)S(1)}, u32[]{:S(2)}, u32[]{:S(2)}) collective-permute-start(bf16[144,512]{1,0:T(8,128)(2,1)S(1)} %collective-permute-done.rest_1_), channel_id=1, source_target_pairs={{0,1},{1,0},{2,3},{3,2},{4,5},{5,4},{6,7},{7,6},{8,9},{9,8},{10,11... | collective-permute-start | bytes 442376 | tf_op jit(solution)/shard_map/ppermute | solution.py:428
  12.0 5.6 %probs_dv.1 = (f32[2,128,512]{2,1,0:T(8,128)S(1)}, f32[2,128,512]{2,1,0:T(8,128)S(1)}, bf16[4,384,1024]{2,1,0:T(8,128)(2,1)S(1)}) custom-call(s32[24]{0:T(128)S(1)} %dynamic-slice_bitcast_fusion.idx_ref, bf16[128,4096]{1,0:T(8,128)(2,1)S(1)} %bitcast.40, bf16[128,4096]{1,0:T(8,128)(2,1)S(1)} %bitcast.42, bf16[144,512]{1,0:T(8,128)(2,1)S(1)} %key_block.1.rest_0_, ...), custom_call_target="tpu_custom_call" | custom-call | flops 805306368 | bytes 8388608 | tf_op jit(solution)/shard_map/probs_dv/pallas_call | solution.py:216
  18.0 2.6 %collective-permute-start.9 = (bf16[256,512]{1,0:T(8,128)(2,1)S(1)}, bf16[256,512]{1,0:T(8,128)(2,1)S(1)}, u32[]{:S(2)}, u32[]{:S(2)}) collective-permute-start(bf16[256,512]{1,0:T(8,128)(2,1)S(1)} %copy-done.4), channel_id=1, source_target_pairs={{0,16},{4,20},{16,24},{20,28},{24,8},{28,12},{8,0},{12,4},{1,17},{... | collective-permute-start | bytes 786440 | tf_op jit(solution)/shard_map/ppermute | solution.py:446
  20.7 1.3 %collective-permute-start.6 = (bf16[2,128,512]{2,1,0:T(8,128)(2,1)S(1)}, bf16[2,128,512]{2,1,0:T(8,128)(2,1)S(1)}, u32[]{:S(2)}, u32[]{:S(2)}) collective-permute-start(bf16[2,128,512]{2,1,0:T(8,128)(2,1)S(1)} %get-tuple-element.64), channel_id=1, source_target_pairs={{0,2},{1,3},{2,0},{3,1},{4,6},{5,7},{6,4},{7,5},{8,10},{9,11},{10,... | collective-permute-start | bytes 786440 | tf_op jit(solution)/shard_map/ppermute | solution.py:428
  23.8 2.2 %split_columns.1 = (bf16[128,2048]{1,0:T(8,128)(2,1)S(1)}, bf16[128,2048]{1,0:T(8,128)(2,1)S(1)}, bf16[128,2048]{1,0:T(8,128)(2,1)S(1)}, bf16[128,2048]{1,0:T(8,128)(2,1)S(1)}) custom-call(s32[24]{0:T(128)S(1)} %dynamic-slice_bitcast_fusion.idx_ref, bf16[128,8192]{1,0:T(8,128)(2,1)} %bitcast.44), custom_call_target="tpu_custom_call" | custom-call | bytes 4194304 | tf_op jit(solution)/shard_map/split_columns/pallas_call | solution.py:71
  26.3 1.5 %collective-permute-start.4 = (bf16[128,2048]{1,0:T(8,128)(2,1)S(1)}, bf16[128,2048]{1,0:T(8,128)(2,1)S(1)}, u32[]{:S(2)}, u32[]{:S(2)}) collective-permute-start(bf16[128,2048]{1,0:T(8,128)(2,1)S(1)} %get-tuple-element.38), channel_id=1, source_target_pairs={{0,1},{1,0},{2,3},{3,2},{4,5},{5,4},{6,7},{7,6},{8,9},{9,8},{10,11... | collective-permute-start | bytes 1572872 | tf_op jit(solution)/shard_map/ppermute | solution.py:428
  29.5 2.6 %collective-permute-start.11 = (bf16[256,512]{1,0:T(8,128)(2,1)S(1)}, bf16[256,512]{1,0:T(8,128)(2,1)S(1)}, u32[]{:S(2)}, u32[]{:S(2)}) collective-permute-start(bf16[256,512]{1,0:T(8,128)(2,1)S(1)} %collective-permute-done.9.rest_6_.rest_2_), channel_id=1, source_target_pairs={{0,16},{4,20},{16,24},{20,28},{24,8},{28,12},{8,0},{12,4},{1,17},{... | collective-permute-start | bytes 786440 | tf_op jit(solution)/shard_map/ppermute | solution.py:446
  32.1 1.9 %collective-permute-done.13.rest_10_.rest_6_ = bf16[256,512]{1,0:T(8,128)(2,1)S(1)} collective-permute-done((bf16[256,512]{1,0:T(8,128)(2,1)S(1)}, bf16[256,512]{1,0:T(8,128)(2,1)S(1)}, u32[]{:S(2)}, u32[]{:S(2)}) %collective-permute-start.13) | collective-permute-done | bytes 262176 | tf_op jit(solution)/shard_map/ppermute | solution.py:446
  34.0 1.8 %collective-permute-start.7 = (bf16[128,2048]{1,0:T(8,128)(2,1)S(1)}, bf16[128,2048]{1,0:T(8,128)(2,1)S(1)}, u32[]{:S(2)}, u32[]{:S(2)}) collective-permute-start(bf16[128,2048]{1,0:T(8,128)(2,1)S(1)} %get-tuple-element.43), channel_id=1, source_target_pairs={{0,3},{1,2},{2,1},{3,0},{4,7},{5,6},{6,5},{7,4},{8,11},{9,10},{10,... | collective-permute-start | bytes 1572872 | tf_op jit(solution)/shard_map/ppermute | solution.py:428
  35.7 1.8 %collective-permute-start.14 = (bf16[256,512]{1,0:T(8,128)(2,1)S(1)}, bf16[256,512]{1,0:T(8,128)(2,1)S(1)}, u32[]{:S(2)}, u32[]{:S(2)}) collective-permute-start(bf16[256,512]{1,0:T(8,128)(2,1)S(1)} %collective-permute-done.13.rest_10_.rest_6_), channel_id=1, source_target_pairs={{0,4},{8,12},{16,20},{24,28},{4,0},{12,8},{20,16},{28,24},{1,5},{9... | collective-permute-start | bytes 786440 | tf_op jit(solution)/shard_map/ppermute | solution.py:449
  37.5 1.3 %collective-permute-done.11.rest_8_.rest_4_ = bf16[256,512]{1,0:T(8,128)(2,1)S(1)} collective-permute-done((bf16[256,512]{1,0:T(8,128)(2,1)S(1)}, bf16[256,512]{1,0:T(8,128)(2,1)S(1)}, u32[]{:S(2)}, u32[]{:S(2)}) %collective-permute-start.11) | collective-permute-done | bytes 262176 | tf_op jit(solution)/shard_map/ppermute | solution.py:446
  38.8 2.0 %collective-permute-start.12 = (bf16[256,512]{1,0:T(8,128)(2,1)S(1)}, bf16[256,512]{1,0:T(8,128)(2,1)S(1)}, u32[]{:S(2)}, u32[]{:S(2)}) collective-permute-start(bf16[256,512]{1,0:T(8,128)(2,1)S(1)} %collective-permute-done.11.rest_8_.rest_4_), channel_id=1, source_target_pairs={{0,4},{8,12},{16,20},{24,28},{4,0},{12,8},{20,16},{28,24},{1,5},{9... | collective-permute-start | bytes 786440 | tf_op jit(solution)/shard_map/ppermute | solution.py:449
  40.9 2.1 %collective-permute-done.14.rest_11_.rest_7_ = bf16[256,512]{1,0:T(8,128)(2,1)S(1)} collective-permute-done((bf16[256,512]{1,0:T(8,128)(2,1)S(1)}, bf16[256,512]{1,0:T(8,128)(2,1)S(1)}, u32[]{:S(2)}, u32[]{:S(2)}) %collective-permute-start.14) | collective-permute-done | bytes 262176 | tf_op jit(solution)/shard_map/ppermute | solution.py:449
  43.0 5.6 %collective-permute-done.12.rest_9_.rest_5_ = bf16[256,512]{1,0:T(8,128)(2,1)S(1)} collective-permute-done((bf16[256,512]{1,0:T(8,128)(2,1)S(1)}, bf16[256,512]{1,0:T(8,128)(2,1)S(1)}, u32[]{:S(2)}, u32[]{:S(2)}) %collective-permute-start.12) | collective-permute-done | bytes 262176 | tf_op jit(solution)/shard_map/ppermute | solution.py:449
  48.6 2.7 %collective-permute-done.7.rest_3_ = bf16[128,2048]{1,0:T(8,128)(2,1)S(1)} collective-permute-done((bf16[128,2048]{1,0:T(8,128)(2,1)S(1)}, bf16[128,2048]{1,0:T(8,128)(2,1)S(1)}, u32[]{:S(2)}, u32[]{:S(2)}) %collective-permute-start.7) | collective-permute-done | bytes 524320 | tf_op jit(solution)/shard_map/ppermute | solution.py:428
  51.3 1.9 %values_part.1 = (f32[2,128,512]{2,1,0:T(8,128)S(1)}, f32[2,128,512]{2,1,0:T(8,128)S(1)}) custom-call(s32[24]{0:T(128)S(1)} %dynamic-slice_bitcast_fusion.idx_ref, bf16[128,2048]{1,0:T(8,128)(2,1)S(1)} %get-tuple-element.34.rest_0_, bf16[128,2048]{1,0:T(8,128)(2,1)S(1)} %collective-permute-done.3.rest_1_, ...), custom_call_target="tpu_custom_call" | custom-call | flops 1073741824 | bytes 8388608 | tf_op jit(solution)/shard_map/values_part/pallas_call | solution.py:319
  55.3 1.3 %collective-permute-start.16 = (bf16[2,128,512]{2,1,0:T(8,128)(2,1)S(1)}, bf16[2,128,512]{2,1,0:T(8,128)(2,1)S(1)}, u32[]{:S(2)}, u32[]{:S(2)}) collective-permute-start(bf16[2,128,512]{2,1,0:T(8,128)(2,1)S(1)} %get-tuple-element.62), channel_id=1, source_target_pairs={{0,2},{1,3},{2,0},{3,1},{4,6},{5,7},{6,4},{7,5},{8,10},{9,11},{10,... | collective-permute-start | bytes 786440 | tf_op jit(solution)/shard_map/ppermute | solution.py:428
  56.6 2.1 %weight_grad_part.1 = (bf16[256,512]{1,0:T(8,128)(2,1)S(1)}, bf16[256,512]{1,0:T(8,128)(2,1)S(1)}, bf16[256,512]{1,0:T(8,128)(2,1)S(1)}, bf16[256,512]{1,0:T(8,1...) custom-call(s32[24]{0:T(128)S(1)} %dynamic-slice_bitcast_fusion.idx_, ...), custom_call_target="tpu_custom_call" | custom-call | flops 1073741824 | bytes 7340032 | tf_op jit(solution)/shard_map/weight_grad_part/pallas_call | solution.py:356
  58.7 1.3 %collective-permute-start.25 = (bf16[256,512]{1,0:T(8,128)(2,1)S(1)}, bf16[256,512]{1,0:T(8,128)(2,1)S(1)}, u32[]{:S(2)}, u32[]{:S(2)}) collective-permute-start(bf16[256,512]{1,0:T(8,128)(2,1)S(1)} %get-tuple-element.56), channel_id=1, source_target_pairs={{0,4},{8,12},{16,20},{24,28},{4,0},{12,8},{20,16},{28,24},{1,5},{9... | collective-permute-start | bytes 786440 | tf_op jit(solution)/shard_map/ppermute | solution.py:449
  60.0 3.1 %collective-permute-done.16 = bf16[2,128,512]{2,1,0:T(8,128)(2,1)S(1)} collective-permute-done((bf16[2,128,512]{2,1,0:T(8,128)(2,1)S(1)}, bf16[2,128,512]{2,1,0:T(8,128)(2,1)S(1)}, u32[]{:S(2)}, u32[]{:S(2)}) %collective-permute-start.16) | collective-permute-done | bytes 262176 | tf_op jit(solution)/shard_map/ppermute | solution.py:428
  64.3 1.2 %collective-permute-start.29 = (bf16[256,512]{1,0:T(8,128)(2,1)S(1)}, bf16[256,512]{1,0:T(8,128)(2,1)S(1)}, u32[]{:S(2)}, u32[]{:S(2)}) collective-permute-start(bf16[256,512]{1,0:T(8,128)(2,1)S(1)} %get-tuple-element.60), channel_id=1, source_target_pairs={{0,4},{8,12},{16,20},{24,28},{4,0},{12,8},{20,16},{28,24},{1,5},{9... | collective-permute-start | bytes 786440 | tf_op jit(solution)/shard_map/ppermute | solution.py:449
  67.0 1.6 %collective-permute-start.26 = (bf16[256,512]{1,0:T(8,128)(2,1)S(1)}, bf16[256,512]{1,0:T(8,128)(2,1)S(1)}, u32[]{:S(2)}, u32[]{:S(2)}) collective-permute-start(bf16[256,512]{1,0:T(8,128)(2,1)S(1)} %fusion.3), channel_id=1, source_target_pairs={{0,16},{4,20},{16,24},{20,28},{24,8},{28,12},{8,0},{12,4},{1,17},{... | collective-permute-start | bytes 786440 | tf_op jit(solution)/shard_map/ppermute | solution.py:446
  68.6 6.1 %scores_dq_dk.1 = (bf16[128,4096]{1,0:T(8,128)(2,1)}, f32[2,128,512]{2,1,0:T(8,128)S(1)}, f32[2,128,512]{2,1,0:T(8,128)S(1)}) custom-call(s32[24]{0:T(128)S(1)} %dynamic-slice_bitcast_fusion.idx_ref, bf16[128,4096]{1,0:T(8,128)(2,1)S(1)} %bitcast.41, bf16[128,4096]{1,0:T(8,128)(2,1)S(1)} %bitcast.43, bf16[4,384,1024]{2,1,0:T(8,128)(2,1)S(1)} %get-tuple-element.33.p_ref, ...), custom_call_target="tpu_custom_call" | custom-call | flops 1207959552 | bytes 10485760 | tf_op jit(solution)/shard_map/scores_dq_dk/pallas_call | solution.py:274
  76.1 1.8 %collective-permute-done.27 = bf16[256,512]{1,0:T(8,128)(2,1)S(1)} collective-permute-done((bf16[256,512]{1,0:T(8,128)(2,1)S(1)}, bf16[256,512]{1,0:T(8,128)(2,1)S(1)}, u32[]{:S(2)}, u32[]{:S(2)}) %collective-permute-start.27) | collective-permute-done | bytes 262176 | tf_op jit(solution)/shard_map/ppermute | solution.py:449
  78.0 1.6 %collective-permute-start.28 = (bf16[256,512]{1,0:T(8,128)(2,1)S(1)}, bf16[256,512]{1,0:T(8,128)(2,1)S(1)}, u32[]{:S(2)}, u32[]{:S(2)}) collective-permute-start(bf16[256,512]{1,0:T(8,128)(2,1)S(1)} %fusion.2), channel_id=1, source_target_pairs={{0,16},{4,20},{16,24},{20,28},{24,8},{28,12},{8,0},{12,4},{1,17},{... | collective-permute-start | bytes 786440 | tf_op jit(solution)/shard_map/ppermute | solution.py:446
  79.6 2.0 %input_grad_part.1 = (bf16[128,2048]{1,0:T(8,128)(2,1)S(1)}, bf16[128,2048]{1,0:T(8,128)(2,1)S(1)}, bf16[128,2048]{1,0:T(8,128)(2,1)S(1)}, bf16[128,2048]{1,0:T(8,128)(2,1)S(1)}) custom-call(s32[24]{0:T(128)S(1)} %dynamic-slice_bitcast_fusion.idx_ref, bf16[2,128,512]{2,1,0:T(8,128)(2,1)S(1)} %add_convert_fusion.g0.rest_4_, ...), custom_call_target="tpu_custom_call" | custom-call | flops 1073741824 | bytes 5242880 | tf_op jit(solution)/shard_map/input_grad_part/pallas_call | solution.py:395
  86.3 4.5 %collective-permute-done.28 = bf16[256,512]{1,0:T(8,128)(2,1)S(1)} collective-permute-done((bf16[256,512]{1,0:T(8,128)(2,1)S(1)}, bf16[256,512]{1,0:T(8,128)(2,1)S(1)}, u32[]{:S(2)}, u32[]{:S(2)}) %collective-permute-start.28) | collective-permute-done | bytes 262176 | tf_op jit(solution)/shard_map/ppermute | solution.py:446
  91.7 1.9 %collective-permute-done.21.rest_1_ = bf16[128,2048]{1,0:T(8,128)(2,1)S(1)} collective-permute-done((bf16[128,2048]{1,0:T(8,128)(2,1)S(1)}, bf16[128,2048]{1,0:T(8,128)(2,1)S(1)}, u32[]{:S(2)}, u32[]{:S(2)}) %collective-permute-start.21) | collective-permute-done | bytes 524320 | tf_op jit(solution)/shard_map/ppermute | solution.py:428
  93.6 14.3 %collective-permute-done.23.rest_3_ = bf16[128,2048]{1,0:T(8,128)(2,1)S(1)} collective-permute-done((bf16[128,2048]{1,0:T(8,128)(2,1)S(1)}, bf16[128,2048]{1,0:T(8,128)(2,1)S(1)}, u32[]{:S(2)}, u32[]{:S(2)}) %collective-permute-start.23) | collective-permute-done | bytes 524320 | tf_op jit(solution)/shard_map/ppermute | solution.py:428
  108.0 2.5 %join_columns.1 = bf16[128,8192]{1,0:T(8,128)(2,1)} custom-call(s32[24]{0:T(128)S(1)} %dynamic-slice_bitcast_fusion.idx_ref, bf16[128,2048]{1,0:T(8,128)(2,1)S(1)} %get-tuple-element.49.rest_0_, bf16[128,2048]{1,0:T(8,128)(2,1)S(1)} %collective-permute-done.21.rest_1_, bf16[128,2048]{1,0:T(8,128)(2,1)S(1)} %collective-permute-done.22.rest_2_, ...), custom_call_target="tpu_custom_call" | custom-call | bytes 4194304 | tf_op jit(solution)/shard_map/join_columns/pallas_call | solution.py:105
  (62 shorter events, 22.2 us)
Async XLA Ops:
  0.6 17.4 %copy-start.4 = (bf16[256,512]{1,0:T(8,128)(2,1)S(1)}, bf16[256,512]{1,0:T(8,128)(2,1)}, u32[]{:S(2)}) copy-start(bf16[256,512]{1,0:T(8,128)(2,1)} %rest_0_.1) | copy-start | bytes 786436
  1.6 5.6 %collective-permute-start = (bf16[144,512]{1,0:T(8,128)(2,1)S(1)}, bf16[144,512]{1,0:T(8,128)(2,1)S(1)}, u32[]{:S(2)}, u32[]{:S(2)}) collective-permute-start(bf16[144,512]{1,0:T(8,128)(2,1)S(1)} %key_block.1.rest_0_), channel_id=1, source_target_pairs={{0,2},{1,3},{2,0},{3,1},{4,6},{5,7},{6,4},{7,5},{8,10},{9,11},{10,... | collective-permute-start | bytes 442376 | tf_op jit(solution)/shard_map/ppermute | solution.py:428
  3.7 5.5 %collective-permute-start.1 = (bf16[144,512]{1,0:T(8,128)(2,1)S(1)}, bf16[144,512]{1,0:T(8,128)(2,1)S(1)}, u32[]{:S(2)}, u32[]{:S(2)}) collective-permute-start(bf16[144,512]{1,0:T(8,128)(2,1)S(1)} %key_block.1.rest_0_), channel_id=1, source_target_pairs={{0,1},{1,0},{2,3},{3,2},{4,5},{5,4},{6,7},{7,6},{8,9},{9,8},{10,11... | collective-permute-start | bytes 442376 | tf_op jit(solution)/shard_map/ppermute | solution.py:428
  7.3 2.3 %collective-permute-start.2 = (bf16[144,512]{1,0:T(8,128)(2,1)S(1)}, bf16[144,512]{1,0:T(8,128)(2,1)S(1)}, u32[]{:S(2)}, u32[]{:S(2)}) collective-permute-start(bf16[144,512]{1,0:T(8,128)(2,1)S(1)} %collective-permute-done.rest_1_), channel_id=1, source_target_pairs={{0,1},{1,0},{2,3},{3,2},{4,5},{5,4},{6,7},{7,6},{8,9},{9,8},{10,11... | collective-permute-start | bytes 442376 | tf_op jit(solution)/shard_map/ppermute | solution.py:428
  17.6 3.0 %collective-permute-start.5 = (f32[2,128,512]{2,1,0:T(8,128)S(1)}, f32[2,128,512]{2,1,0:T(8,128)S(1)}, u32[]{:S(2)}, u32[]{:S(2)}) collective-permute-start(f32[2,128,512]{2,1,0:T(8,128)S(1)} %get-tuple-element.42), channel_id=1, source_target_pairs={{0,1},{1,0},{2,3},{3,2},{4,5},{5,4},{6,7},{7,6},{8,9},{9,8},{10,11... | collective-permute-start | bytes 1572872 | tf_op jit(solution)/shard_map/ppermute | solution.py:428
  18.0 8.2 %collective-permute-start.9 = (bf16[256,512]{1,0:T(8,128)(2,1)S(1)}, bf16[256,512]{1,0:T(8,128)(2,1)S(1)}, u32[]{:S(2)}, u32[]{:S(2)}) collective-permute-start(bf16[256,512]{1,0:T(8,128)(2,1)S(1)} %copy-done.4), channel_id=1, source_target_pairs={{0,16},{4,20},{16,24},{20,28},{24,8},{28,12},{8,0},{12,4},{1,17},{... | collective-permute-start | bytes 786440 | tf_op jit(solution)/shard_map/ppermute | solution.py:446
  20.7 7.5 %collective-permute-start.6 = (bf16[2,128,512]{2,1,0:T(8,128)(2,1)S(1)}, bf16[2,128,512]{2,1,0:T(8,128)(2,1)S(1)}, u32[]{:S(2)}, u32[]{:S(2)}) collective-permute-start(bf16[2,128,512]{2,1,0:T(8,128)(2,1)S(1)} %get-tuple-element.64), channel_id=1, source_target_pairs={{0,2},{1,3},{2,0},{3,1},{4,6},{5,7},{6,4},{7,5},{8,10},{9,11},{10,... | collective-permute-start | bytes 786440 | tf_op jit(solution)/shard_map/ppermute | solution.py:428
  22.0 7.5 %collective-permute-start.8 = (bf16[256,512]{1,0:T(8,128)(2,1)S(1)}, bf16[256,512]{1,0:T(8,128)(2,1)S(1)}, u32[]{:S(2)}, u32[]{:S(2)}) collective-permute-start(bf16[256,512]{1,0:T(8,128)(2,1)S(1)} %copy-done.4), channel_id=1, source_target_pairs={{0,4},{8,12},{16,20},{24,28},{4,0},{12,8},{20,16},{28,24},{1,5},{9... | collective-permute-start | bytes 786440 | tf_op jit(solution)/shard_map/ppermute | solution.py:449
  23.2 10.8 %collective-permute-start.13 = (bf16[256,512]{1,0:T(8,128)(2,1)S(1)}, bf16[256,512]{1,0:T(8,128)(2,1)S(1)}, u32[]{:S(2)}, u32[]{:S(2)}) collective-permute-start(bf16[256,512]{1,0:T(8,128)(2,1)S(1)} %copy-done.4), channel_id=1, source_target_pairs={{16,0},{20,4},{24,16},{28,20},{8,24},{12,28},{0,8},{4,12},{17,1},{... | collective-permute-start | bytes 786440 | tf_op jit(solution)/shard_map/ppermute | solution.py:446
  25.9 17.0 %collective-permute-start.3 = (bf16[128,2048]{1,0:T(8,128)(2,1)S(1)}, bf16[128,2048]{1,0:T(8,128)(2,1)S(1)}, u32[]{:S(2)}, u32[]{:S(2)}) collective-permute-start(bf16[128,2048]{1,0:T(8,128)(2,1)S(1)} %get-tuple-element.36), channel_id=1, source_target_pairs={{0,2},{1,3},{2,0},{3,1},{4,6},{5,7},{6,4},{7,5},{8,10},{9,11},{10,... | collective-permute-start | bytes 1572872 | tf_op jit(solution)/shard_map/ppermute | solution.py:428
  26.3 16.7 %collective-permute-start.4 = (bf16[128,2048]{1,0:T(8,128)(2,1)S(1)}, bf16[128,2048]{1,0:T(8,128)(2,1)S(1)}, u32[]{:S(2)}, u32[]{:S(2)}) collective-permute-start(bf16[128,2048]{1,0:T(8,128)(2,1)S(1)} %get-tuple-element.38), channel_id=1, source_target_pairs={{0,1},{1,0},{2,3},{3,2},{4,5},{5,4},{6,7},{7,6},{8,9},{9,8},{10,11... | collective-permute-start | bytes 1572872 | tf_op jit(solution)/shard_map/ppermute | solution.py:428
  28.2 7.5 %collective-permute-start.10 = (bf16[256,512]{1,0:T(8,128)(2,1)S(1)}, bf16[256,512]{1,0:T(8,128)(2,1)S(1)}, u32[]{:S(2)}, u32[]{:S(2)}) collective-permute-start(bf16[256,512]{1,0:T(8,128)(2,1)S(1)} %collective-permute-done.9.rest_6_.rest_2_), channel_id=1, source_target_pairs={{0,4},{8,12},{16,20},{24,28},{4,0},{12,8},{20,16},{28,24},{1,5},{9... | collective-permute-start | bytes 786440 | tf_op jit(solution)/shard_map/ppermute | solution.py:449
  29.5 9.4 %collective-permute-start.11 = (bf16[256,512]{1,0:T(8,128)(2,1)S(1)}, bf16[256,512]{1,0:T(8,128)(2,1)S(1)}, u32[]{:S(2)}, u32[]{:S(2)}) collective-permute-start(bf16[256,512]{1,0:T(8,128)(2,1)S(1)} %collective-permute-done.9.rest_6_.rest_2_), channel_id=1, source_target_pairs={{0,16},{4,20},{16,24},{20,28},{24,8},{28,12},{8,0},{12,4},{1,17},{... | collective-permute-start | bytes 786440 | tf_op jit(solution)/shard_map/ppermute | solution.py:446
  34.0 17.3 %collective-permute-start.7 = (bf16[128,2048]{1,0:T(8,128)(2,1)S(1)}, bf16[128,2048]{1,0:T(8,128)(2,1)S(1)}, u32[]{:S(2)}, u32[]{:S(2)}) collective-permute-start(bf16[128,2048]{1,0:T(8,128)(2,1)S(1)} %get-tuple-element.43), channel_id=1, source_target_pairs={{0,3},{1,2},{2,1},{3,0},{4,7},{5,6},{6,5},{7,4},{8,11},{9,10},{10,... | collective-permute-start | bytes 1572872 | tf_op jit(solution)/shard_map/ppermute | solution.py:428
  35.7 7.2 %collective-permute-start.14 = (bf16[256,512]{1,0:T(8,128)(2,1)S(1)}, bf16[256,512]{1,0:T(8,128)(2,1)S(1)}, u32[]{:S(2)}, u32[]{:S(2)}) collective-permute-start(bf16[256,512]{1,0:T(8,128)(2,1)S(1)} %collective-permute-done.13.rest_10_.rest_6_), channel_id=1, source_target_pairs={{0,4},{8,12},{16,20},{24,28},{4,0},{12,8},{20,16},{28,24},{1,5},{9... | collective-permute-start | bytes 786440 | tf_op jit(solution)/shard_map/ppermute | solution.py:449
  38.8 9.8 %collective-permute-start.12 = (bf16[256,512]{1,0:T(8,128)(2,1)S(1)}, bf16[256,512]{1,0:T(8,128)(2,1)S(1)}, u32[]{:S(2)}, u32[]{:S(2)}) collective-permute-start(bf16[256,512]{1,0:T(8,128)(2,1)S(1)} %collective-permute-done.11.rest_8_.rest_4_), channel_id=1, source_target_pairs={{0,4},{8,12},{16,20},{24,28},{4,0},{12,8},{20,16},{28,24},{1,5},{9... | collective-permute-start | bytes 786440 | tf_op jit(solution)/shard_map/ppermute | solution.py:449
  53.2 2.0 %collective-permute-start.15 = (f32[2,128,512]{2,1,0:T(8,128)S(1)}, f32[2,128,512]{2,1,0:T(8,128)S(1)}, u32[]{:S(2)}, u32[]{:S(2)}) collective-permute-start(f32[2,128,512]{2,1,0:T(8,128)S(1)} %get-tuple-element.45), channel_id=1, source_target_pairs={{0,1},{1,0},{2,3},{3,2},{4,5},{5,4},{6,7},{7,6},{8,9},{9,8},{10,11... | collective-permute-start | bytes 1572872 | tf_op jit(solution)/shard_map/ppermute | solution.py:428
  53.4 3.2 %collective-permute-start.20 = (bf16[2,128,512]{2,1,0:T(8,128)(2,1)S(1)}, bf16[2,128,512]{2,1,0:T(8,128)(2,1)S(1)}, u32[]{:S(2)}, u32[]{:S(2)}) collective-permute-start(bf16[2,128,512]{2,1,0:T(8,128)(2,1)S(1)} %add_convert_fusion.g0.rest_4_), channel_id=1, source_target_pairs={{0,1},{1,0},{2,3},{3,2},{4,5},{5,4},{6,7},{7,6},{8,9},{9,8},{10,11... | collective-permute-start | bytes 786440 | tf_op jit(solution)/shard_map/ppermute | solution.py:428
  55.3 7.8 %collective-permute-start.16 = (bf16[2,128,512]{2,1,0:T(8,128)(2,1)S(1)}, bf16[2,128,512]{2,1,0:T(8,128)(2,1)S(1)}, u32[]{:S(2)}, u32[]{:S(2)}) collective-permute-start(bf16[2,128,512]{2,1,0:T(8,128)(2,1)S(1)} %get-tuple-element.62), channel_id=1, source_target_pairs={{0,2},{1,3},{2,0},{3,1},{4,6},{5,7},{6,4},{7,5},{8,10},{9,11},{10,... | collective-permute-start | bytes 786440 | tf_op jit(solution)/shard_map/ppermute | solution.py:428
  58.7 8.3 %collective-permute-start.25 = (bf16[256,512]{1,0:T(8,128)(2,1)S(1)}, bf16[256,512]{1,0:T(8,128)(2,1)S(1)}, u32[]{:S(2)}, u32[]{:S(2)}) collective-permute-start(bf16[256,512]{1,0:T(8,128)(2,1)S(1)} %get-tuple-element.56), channel_id=1, source_target_pairs={{0,4},{8,12},{16,20},{24,28},{4,0},{12,8},{20,16},{28,24},{1,5},{9... | collective-permute-start | bytes 786440 | tf_op jit(solution)/shard_map/ppermute | solution.py:449
  63.2 5.4 %collective-permute-start.17 = (bf16[2,128,512]{2,1,0:T(8,128)(2,1)S(1)}, bf16[2,128,512]{2,1,0:T(8,128)(2,1)S(1)}, u32[]{:S(2)}, u32[]{:S(2)}) collective-permute-start(bf16[2,128,512]{2,1,0:T(8,128)(2,1)S(1)} %add_convert_fusion.1.v0_ref), channel_id=1, source_target_pairs={{0,1},{1,0},{2,3},{3,2},{4,5},{5,4},{6,7},{7,6},{8,9},{9,8},{10,11... | collective-permute-start | bytes 786440 | tf_op jit(solution)/shard_map/ppermute | solution.py:428
  64.3 11.7 %collective-permute-start.29 = (bf16[256,512]{1,0:T(8,128)(2,1)S(1)}, bf16[256,512]{1,0:T(8,128)(2,1)S(1)}, u32[]{:S(2)}, u32[]{:S(2)}) collective-permute-start(bf16[256,512]{1,0:T(8,128)(2,1)S(1)} %get-tuple-element.60), channel_id=1, source_target_pairs={{0,4},{8,12},{16,20},{24,28},{4,0},{12,8},{20,16},{28,24},{1,5},{9... | collective-permute-start | bytes 786440 | tf_op jit(solution)/shard_map/ppermute | solution.py:449
  65.5 12.4 %collective-permute-start.27 = (bf16[256,512]{1,0:T(8,128)(2,1)S(1)}, bf16[256,512]{1,0:T(8,128)(2,1)S(1)}, u32[]{:S(2)}, u32[]{:S(2)}) collective-permute-start(bf16[256,512]{1,0:T(8,128)(2,1)S(1)} %get-tuple-element.58), channel_id=1, source_target_pairs={{0,4},{8,12},{16,20},{24,28},{4,0},{12,8},{20,16},{28,24},{1,5},{9... | collective-permute-start | bytes 786440 | tf_op jit(solution)/shard_map/ppermute | solution.py:449
  65.7 17.8 %collective-permute-start.24 = (bf16[256,512]{1,0:T(8,128)(2,1)S(1)}, bf16[256,512]{1,0:T(8,128)(2,1)S(1)}, u32[]{:S(2)}, u32[]{:S(2)}) collective-permute-start(bf16[256,512]{1,0:T(8,128)(2,1)S(1)} %get-tuple-element.54), channel_id=1, source_target_pairs={{0,4},{8,12},{16,20},{24,28},{4,0},{12,8},{20,16},{28,24},{1,5},{9... | collective-permute-start | bytes 786440 | tf_op jit(solution)/shard_map/ppermute | solution.py:449
  67.0 10.8 %collective-permute-start.26 = (bf16[256,512]{1,0:T(8,128)(2,1)S(1)}, bf16[256,512]{1,0:T(8,128)(2,1)S(1)}, u32[]{:S(2)}, u32[]{:S(2)}) collective-permute-start(bf16[256,512]{1,0:T(8,128)(2,1)S(1)} %fusion.3), channel_id=1, source_target_pairs={{0,16},{4,20},{16,24},{20,28},{24,8},{28,12},{8,0},{12,4},{1,17},{... | collective-permute-start | bytes 786440 | tf_op jit(solution)/shard_map/ppermute | solution.py:446
  74.7 10.0 %collective-permute-start.18 = (f32[2,128,512]{2,1,0:T(8,128)S(1)}, f32[2,128,512]{2,1,0:T(8,128)S(1)}, u32[]{:S(2)}, u32[]{:S(2)}) collective-permute-start(f32[2,128,512]{2,1,0:T(8,128)S(1)} %get-tuple-element.48), channel_id=1, source_target_pairs={{0,1},{1,0},{2,3},{3,2},{4,5},{5,4},{6,7},{7,6},{8,9},{9,8},{10,11... | collective-permute-start | bytes 1572872 | tf_op jit(solution)/shard_map/ppermute | solution.py:428
  76.0 9.4 %collective-permute-start.30 = (bf16[256,512]{1,0:T(8,128)(2,1)S(1)}, bf16[256,512]{1,0:T(8,128)(2,1)S(1)}, u32[]{:S(2)}, u32[]{:S(2)}) collective-permute-start(bf16[256,512]{1,0:T(8,128)(2,1)S(1)} %fusion), channel_id=1, source_target_pairs={{16,0},{20,4},{24,16},{28,20},{8,24},{12,28},{0,8},{4,12},{17,1},{... | collective-permute-start | bytes 786440 | tf_op jit(solution)/shard_map/ppermute | solution.py:446
  78.0 12.8 %collective-permute-start.28 = (bf16[256,512]{1,0:T(8,128)(2,1)S(1)}, bf16[256,512]{1,0:T(8,128)(2,1)S(1)}, u32[]{:S(2)}, u32[]{:S(2)}) collective-permute-start(bf16[256,512]{1,0:T(8,128)(2,1)S(1)} %fusion.2), channel_id=1, source_target_pairs={{0,16},{4,20},{16,24},{20,28},{24,8},{28,12},{8,0},{12,4},{1,17},{... | collective-permute-start | bytes 786440 | tf_op jit(solution)/shard_map/ppermute | solution.py:446
  81.6 12.0 %collective-permute-start.21 = (bf16[128,2048]{1,0:T(8,128)(2,1)S(1)}, bf16[128,2048]{1,0:T(8,128)(2,1)S(1)}, u32[]{:S(2)}, u32[]{:S(2)}) collective-permute-start(bf16[128,2048]{1,0:T(8,128)(2,1)S(1)} %get-tuple-element.50), channel_id=1, source_target_pairs={{0,2},{1,3},{2,0},{3,1},{4,6},{5,7},{6,4},{7,5},{8,10},{9,11},{10,... | collective-permute-start | bytes 1572872 | tf_op jit(solution)/shard_map/ppermute | solution.py:428
  83.5 10.1 %collective-permute-start.22 = (bf16[128,2048]{1,0:T(8,128)(2,1)S(1)}, bf16[128,2048]{1,0:T(8,128)(2,1)S(1)}, u32[]{:S(2)}, u32[]{:S(2)}) collective-permute-start(bf16[128,2048]{1,0:T(8,128)(2,1)S(1)} %get-tuple-element.51), channel_id=1, source_target_pairs={{0,1},{1,0},{2,3},{3,2},{4,5},{5,4},{6,7},{7,6},{8,9},{9,8},{10,11... | collective-permute-start | bytes 1572872 | tf_op jit(solution)/shard_map/ppermute | solution.py:428
  84.7 23.3 %collective-permute-start.23 = (bf16[128,2048]{1,0:T(8,128)(2,1)S(1)}, bf16[128,2048]{1,0:T(8,128)(2,1)S(1)}, u32[]{:S(2)}, u32[]{:S(2)}) collective-permute-start(bf16[128,2048]{1,0:T(8,128)(2,1)S(1)} %get-tuple-element.53), channel_id=1, source_target_pairs={{0,3},{1,2},{2,1},{3,0},{4,7},{5,6},{6,5},{7,4},{8,11},{9,10},{10,... | collective-permute-start | bytes 1572872 | tf_op jit(solution)/shard_map/ppermute | solution.py:428
  85.4 25.1 %collective-permute-start.19 = (bf16[128,512]{1,0:T(8,128)(2,1)S(1)}, bf16[128,512]{1,0:T(8,128)(2,1)S(1)}, u32[]{:S(2)}, u32[]{:S(2)}) collective-permute-start(bf16[128,512]{1,0:T(8,128)(2,1)S(1)} %fusion.9), channel_id=1, source_target_pairs={{0,2},{1,3},{2,0},{3,1},{4,6},{5,7},{6,4},{7,5},{8,10},{9,11},{10,... | collective-permute-start | bytes 393224 | tf_op jit(solution)/shard_map/ppermute | solution.py:428
  (4 other events, 22.4 us)

commit v2 on v0

--- a/solution.py
+++ b/solution.py
@@ -41,8 +41,21 @@
     return max(1, min(4, dp * width // 128 // 2))
 
 
-def split_kernel(sp, steps, reps, width, base, idx_ref, x_ref, *rest):
-    outs, (hold, part, sems) = rest[:sp], rest[sp:]
+def piece_layout(sp, steps, cols):
+    nx, out = sp // 2, []
+    for r in range(sp):
+        count = 2 if r % nx and r // nx and steps % 2 == 0 else 1
+        out += [(r, i * cols // count, cols // count) for i in range(count)]
+    return out
+
+
+def fill_columns(layout, xs, x_hold, tok):
+    for (r, at, size), x in zip(layout, xs):
+        x_hold[r * tok : (r + 1) * tok, at : at + size] = x[...]
+
+
+def split_kernel(sp, layout, steps, reps, width, base, idx_ref, x_ref, *rest):
+    outs, (hold, part, sems) = rest[: len(layout)], rest[len(layout) :]
     block = reps * width
     copies = [
         pltpu.make_async_copy(
@@ -59,20 +72,21 @@
                 part[a, :, d * width : (d + 1) * width] = hold[
                     i, :, (d * sp + a) * width : (d * sp + a + 1) * width
                 ]
-        for r in range(sp):
-            outs[r][:, i * block : (i + 1) * block] = part[idx_ref[base + r]]
-
-
-def split_columns(idx, base, x, sp, dp, width):
+        for (r, at, size), out in zip(layout, outs):
+            if at <= i * block < at + size:
+                out[:, i * block - at : (i + 1) * block - at] = part[idx_ref[base + r]]
+
+
+def split_columns(idx, base, x, layout, sp, dp, width):
     tok = x.shape[0]
     steps = column_steps(dp, width)
     reps = dp // steps
     block = reps * width
     return pl.pallas_call(
-        functools.partial(split_kernel, sp, steps, reps, width, base),
-        out_shape=[jax.ShapeDtypeStruct((tok, dp * width), BF)] * sp,
+        functools.partial(split_kernel, sp, layout, steps, reps, width, base),
+        out_shape=[jax.ShapeDtypeStruct((tok, size), BF) for _, _, size in layout],
         in_specs=[SM, HB],
-        out_specs=[VM] * sp,
+        out_specs=[VM] * len(layout),
         scratch_shapes=[
             pltpu.VMEM((steps, tok, sp * block), BF),
             pltpu.VMEM((sp, tok, block), BF),
@@ -306,28 +320,27 @@
     )(idx, q, g, lse, v0, v1, *kds)
 
 
-def values_kernel(sp, dp, tok, width, base, idx_ref, *rest):
-    nx = sp // 2
-    xs, ws = rest[:sp], rest[sp : sp + dp]
-    keep, send, x_hold, w_hold = rest[sp + dp :]
+def values_kernel(sp, dp, layout, tok, width, base, idx_ref, *rest):
+    nx, count = sp // 2, len(layout)
+    xs, ws = rest[:count], rest[count : count + dp]
+    keep, send, x_hold, w_hold = rest[count + dp :]
     for i in range(dp):
         w_hold[rows_at(idx_ref[base + i], width), :] = ws[i][...]
-    for r in range(sp):
-        x_hold[r * tok : (r + 1) * tok, :] = xs[r][...]
+    fill_columns(layout, xs, x_hold, tok)
     out = dot(x_hold[...], w_hold[...], NN)
     for dx in range(nx):
         keep[dx] = out[dx * tok : (dx + 1) * tok]
         send[dx] = out[(nx + dx) * tok : (nx + dx + 1) * tok]
 
 
-def values_call(idx, base, xs, ws, sp, dp, tok, width):
+def values_call(idx, base, xs, ws, layout, sp, dp, tok, width):
     nx, kv = sp // 2, ws[0].shape[1]
     cols = dp * width
     part = jax.ShapeDtypeStruct((nx, tok, kv), F32)
     return pl.pallas_call(
-        functools.partial(values_kernel, sp, dp, tok, width, base),
+        functools.partial(values_kernel, sp, dp, layout, tok, width, base),
         out_shape=[part, part],
-        in_specs=[SM] + [VM] * (sp + dp),
+        in_specs=[SM] + [VM] * (len(xs) + dp),
         out_specs=[VM] * 2,
         scratch_shapes=[pltpu.VMEM((sp * tok, cols), BF), pltpu.VMEM((cols, kv), BF)],
         compiler_params=grant(16),
@@ -338,15 +351,15 @@
     )(idx, *xs, *ws)
 
 
-def wgrad_kernel(sp, nz, ny, tok, width, base, idx_ref, *rest):
-    nx = sp // 2
-    xs, (g0, g1) = rest[:sp], rest[sp : sp + 2]
-    outs = rest[sp + 2 : sp + 2 + 2 * nz]
-    x_hold, g_hold, total = rest[sp + 2 + 2 * nz :]
+def wgrad_kernel(sp, nz, ny, layout, tok, width, base, idx_ref, *rest):
+    nx, count = sp // 2, len(layout)
+    xs, (g0, g1) = rest[:count], rest[count : count + 2]
+    outs = rest[count + 2 : count + 2 + 2 * nz]
+    x_hold, g_hold, total = rest[count + 2 + 2 * nz :]
+    fill_columns(layout, xs, x_hold, tok)
     for dx in range(nx):
         for core, src in ((0, g0), (1, g1)):
             r = core * nx + dx
-            x_hold[r * tok : (r + 1) * tok, :] = xs[r][...]
             g_hold[r * tok : (r + 1) * tok, :] = src[dx]
     cols = x_hold.shape[1]
     step = min(cols, 512)
@@ -358,14 +371,14 @@
             outs[nz + k][j - 1] = total[rows_at(idx_ref[base + k * ny + j], width), :]
 
 
-def wgrad_call(idx, base, xs, g0, g1, sp, nz, ny, tok, width):
+def wgrad_call(idx, base, xs, g0, g1, layout, sp, nz, ny, tok, width):
     kv = g0.shape[2]
     cols = nz * ny * width
     return pl.pallas_call(
-        functools.partial(wgrad_kernel, sp, nz, ny, tok, width, base),
+        functools.partial(wgrad_kernel, sp, nz, ny, layout, tok, width, base),
         out_shape=[jax.ShapeDtypeStruct((width, kv), BF)] * nz
         + [jax.ShapeDtypeStruct((ny - 1, width, kv), F32)] * nz,
-        in_specs=[SM] + [VM] * (sp + 2),
+        in_specs=[SM] + [VM] * (len(xs) + 2),
         out_specs=[VM] * (2 * nz),
         scratch_shapes=[
             pltpu.VMEM((sp * tok, cols), BF),
@@ -497,7 +510,8 @@
             if j + 1 < ny:
                 v = send_y(v)
 
-    pieces = split_columns(idx, at_fwd, layer_input[0], sp, dp, width)
+    layout = piece_layout(sp, column_steps(dp, width), dp * width)
+    pieces = split_columns(idx, at_fwd, layer_input[0], layout, sp, dp, width)
     ready = [pieces[0]] + [after(v, near[-1]) for v in pieces[1:]]
 
     dv_keep, dv_send, lse = probs_call(idx, q, g, kds, sp, tok, win, kvh, group)
@@ -515,16 +529,16 @@
         mine = total.astype(BF)
         return mine, send_sp(mine, 0, 1), got
 
-    vg0, vg1, _ = reduce_all(dv_keep, dv_send)
+    vg0, vg1, vg_got = reduce_all(dv_keep, dv_send)
 
     xs = [pieces[0]]
-    for r in range(1, sp):
+    for (r, at, _), v in list(zip(layout, ready))[1:]:
         dx, dc = r % nx, r // nx
-        xs.append(send_sp(ready[r], dx, dc))
+        xs.append(send_sp(after(v, vg_got) if at else v, dx, dc))
 
     parts = igrad_call(idx, at_gather, vg0, vg1, rows, sp, dp, tok, width)
 
-    blocks = wgrad_call(idx, at_scatter, xs, vg0, vg1, sp, nz, ny, tok, width)
+    blocks = wgrad_call(idx, at_scatter, xs, vg0, vg1, layout, sp, nz, ny, tok, width)
     lines = {}
     for i, k in enumerate(to_z):
         line = blocks[i]
@@ -540,7 +554,7 @@
         if run is not None:
             weight_grad = weight_grad + run
 
-    v_keep, v_send = values_call(idx, at_gather, xs, rows, sp, dp, tok, width)
+    v_keep, v_send = values_call(idx, at_gather, xs, rows, layout, sp, dp, tok, width)
     v0, v1, v_got = reduce_all(v_keep, v_send)
     dq, dk_keep, dk_send = scores_call(idx, q, g, lse, v0, v1, kds, sp, tok, win, kvh, group)
     dk = reduce_core(dk_keep, dk_send)

time: 105 us -> 121 us (1.15)
  the two profiles are of different devices: /device:TPU:0 before, /device:TPU:1 now
where the time goes in v2:
time: 121 us
  waiting for transfers between devices  57.4 us (47%)
  starting transfers between devices  34.3 us (28%)
  Pallas kernels  23 us (19%)
  local copies, waits for them, and re-layouts  3.21 us (3%)
  other arithmetic  2.28 us (2%)
    ppermute x18, waiting for transfers between devices, send_sp(): return lax.ppermute(v, 'sp', sp_perm(dx % nx, dc))  33.6 us
    ppermute x18, starting transfers between devices, send_sp(): return lax.ppermute(v, 'sp', sp_perm(dx % nx, dc))  20.9 us
    ppermute x8, waiting for transfers between devices, send_y(): return lax.ppermute(v, 'dp', y_next)  12.9 us
    ppermute x6, waiting for transfers between devices, send_z(): return lax.ppermute(v, 'dp', z_next if forward else z_back)  10.8 us
    ppermute x6, starting transfers between devices, send_z(): return lax.ppermute(v, 'dp', z_next if forward else z_back)  7.45 us
    pallas_call x1, Pallas kernels, scores_call(): pl.pallas_call(functools.partial(scores_kernel, sp, tok, win, group, pair...  6.39 us
    ppermute x8, starting transfers between devices, send_y(): return lax.ppermute(v, 'dp', y_next)  5.93 us
    pallas_call x1, Pallas kernels, probs_call(): pl.pallas_call(functools.partial(probs_kernel, sp, tok, win, group, pair)...  4.96 us
  transfers between devices with their start and end apart: 32, of which 13 were waited for; matrix products, arithmetic and copies ran while one was open for 2% of the time, Pallas kernels for 13%

profile of v2, /device:TPU:1, one launch (start us, length us, event | category | flops | bytes accessed | tf_op | source)
XLA Modules:
  0.0 121.0 jit_solution(17893703437721009693)
XLA Ops:
  1.6 2.1 %collective-permute-start = (bf16[144,512]{1,0:T(8,128)(2,1)S(1)}, bf16[144,512]{1,0:T(8,128)(2,1)S(1)}, u32[]{:S(2)}, u32[]{:S(2)}) collective-permute-start(bf16[144,512]{1,0:T(8,128)(2,1)S(1)} %key_block.1.rest_0_), channel_id=1, source_target_pairs={{0,2},{1,3},{2,0},{3,1},{4,6},{5,7},{6,4},{7,5},{8,10},{9,11},{10,... | collective-permute-start | bytes 442376 | tf_op jit(solution)/shard_map/ppermute | solution.py:449
  4.7 2.6 %collective-permute-done.rest_1_ = bf16[144,512]{1,0:T(8,128)(2,1)S(1)} collective-permute-done((bf16[144,512]{1,0:T(8,128)(2,1)S(1)}, bf16[144,512]{1,0:T(8,128)(2,1)S(1)}, u32[]{:S(2)}, u32[]{:S(2)}) %collective-permute-start) | collective-permute-done | bytes 147488 | tf_op jit(solution)/shard_map/ppermute | solution.py:449
  7.3 1.3 %collective-permute-start.2 = (bf16[144,512]{1,0:T(8,128)(2,1)S(1)}, bf16[144,512]{1,0:T(8,128)(2,1)S(1)}, u32[]{:S(2)}, u32[]{:S(2)}) collective-permute-start(bf16[144,512]{1,0:T(8,128)(2,1)S(1)} %collective-permute-done.rest_1_), channel_id=1, source_target_pairs={{0,1},{1,0},{2,3},{3,2},{4,5},{5,4},{6,7},{7,6},{8,9},{9,8},{10,11... | collective-permute-start | bytes 442376 | tf_op jit(solution)/shard_map/ppermute | solution.py:449
  12.0 5.0 %probs_dv.1 = (f32[2,128,512]{2,1,0:T(8,128)S(1)}, f32[2,128,512]{2,1,0:T(8,128)S(1)}, f32[32,128]{1,0:T(8,128)S(1)}) custom-call(s32[24]{0:T(128)S(1)} %dynamic-slice_bitcast_fusion.idx_ref, bf16[128,4096]{1,0:T(8,128)(2,1)S(1)} %bitcast.40, bf16[128,4096]{1,0:T(8,128)(2,1)S(1)} %bitcast.42, bf16[144,512]{1,0:T(8,128)(2,1)S(1)} %key_block.1.rest_0_, ...), custom_call_target="tpu_custom_call" | custom-call | flops 805306368 | bytes 8388608 | tf_op jit(solution)/shard_map/probs_dv/pallas_call | solution.py:230
  17.4 2.6 %collective-permute-start.10 = (bf16[256,512]{1,0:T(8,128)(2,1)S(1)}, bf16[256,512]{1,0:T(8,128)(2,1)S(1)}, u32[]{:S(2)}, u32[]{:S(2)}) collective-permute-start(bf16[256,512]{1,0:T(8,128)(2,1)S(1)} %copy-done), channel_id=1, source_target_pairs={{0,16},{4,20},{16,24},{20,28},{24,8},{28,12},{8,0},{12,4},{1,17},{... | collective-permute-start | bytes 786440 | tf_op jit(solution)/shard_map/ppermute | solution.py:467
  19.9 1.2 %collective-permute-start.9 = (bf16[256,512]{1,0:T(8,128)(2,1)S(1)}, bf16[256,512]{1,0:T(8,128)(2,1)S(1)}, u32[]{:S(2)}, u32[]{:S(2)}) collective-permute-start(bf16[256,512]{1,0:T(8,128)(2,1)S(1)} %copy-done), channel_id=1, source_target_pairs={{0,4},{8,12},{16,20},{24,28},{4,0},{12,8},{20,16},{28,24},{1,5},{9... | collective-permute-start | bytes 786440 | tf_op jit(solution)/shard_map/ppermute | solution.py:470
  21.3 1.3 %collective-permute-start.7 = (bf16[2,128,512]{2,1,0:T(8,128)(2,1)S(1)}, bf16[2,128,512]{2,1,0:T(8,128)(2,1)S(1)}, u32[]{:S(2)}, u32[]{:S(2)}) collective-permute-start(bf16[2,128,512]{2,1,0:T(8,128)(2,1)S(1)} %get-tuple-element.68), channel_id=1, source_target_pairs={{0,2},{1,3},{2,0},{3,1},{4,6},{5,7},{6,4},{7,5},{8,10},{9,11},{10,... | collective-permute-start | bytes 786440 | tf_op jit(solution)/shard_map/ppermute | solution.py:449
  22.6 2.2 %split_columns.1 = (bf16[128,2048]{1,0:T(8,128)(2,1)S(1)}, bf16[128,2048]{1,0:T(8,128)(2,1)S(1)}, bf16[128,2048]{1,0:T(8,128)(2,1)S(1)}, bf16[128,1024]{1,0:T(8,128)(2,1)S(1)}, bf16[128,1024]{1,0:T(8,128)(2,1)S(1)}) custom-call(s32[24]{0:T(128)S(1)} %dynamic-slice_bitcast_fusion.idx_ref, bf16[128,8192]{1,0:T(8,128)(2,1)} %bitcast.44), custom_call_target="tpu_custom_call" | custom-call | bytes 4194304 | tf_op jit(solution)/shard_map/split_columns/pallas_call | solution.py:85
  25.5 2.7 %collective-permute-start.5 = (bf16[128,1024]{1,0:T(8,128)(2,1)S(1)}, bf16[128,1024]{1,0:T(8,128)(2,1)S(1)}, u32[]{:S(2)}, u32[]{:S(2)}) collective-permute-start(bf16[128,1024]{1,0:T(8,128)(2,1)S(1)} %get-tuple-element.42), channel_id=1, source_target_pairs={{0,3},{1,2},{2,1},{3,0},{4,7},{5,6},{6,5},{7,4},{8,11},{9,10},{10,... | collective-permute-start | bytes 786440 | tf_op jit(solution)/shard_map/ppermute | solution.py:449
  28.2 5.2 %collective-permute-done.14.rest_11_.rest_6_ = bf16[256,512]{1,0:T(8,128)(2,1)S(1)} collective-permute-done((bf16[256,512]{1,0:T(8,128)(2,1)S(1)}, bf16[256,512]{1,0:T(8,128)(2,1)S(1)}, u32[]{:S(2)}, u32[]{:S(2)}) %collective-permute-start.14) | collective-permute-done | bytes 262176 | tf_op jit(solution)/shard_map/ppermute | solution.py:467
  33.4 1.2 %collective-permute-start.11 = (bf16[256,512]{1,0:T(8,128)(2,1)S(1)}, bf16[256,512]{1,0:T(8,128)(2,1)S(1)}, u32[]{:S(2)}, u32[]{:S(2)}) collective-permute-start(bf16[256,512]{1,0:T(8,128)(2,1)S(1)} %collective-permute-done.10.rest_7_.rest_2_), channel_id=1, source_target_pairs={{0,4},{8,12},{16,20},{24,28},{4,0},{12,8},{20,16},{28,24},{1,5},{9... | collective-permute-start | bytes 786440 | tf_op jit(solution)/shard_map/ppermute | solution.py:470
  34.6 1.4 %collective-permute-start.4 = (bf16[128,2048]{1,0:T(8,128)(2,1)S(1)}, bf16[128,2048]{1,0:T(8,128)(2,1)S(1)}, u32[]{:S(2)}, u32[]{:S(2)}) collective-permute-start(bf16[128,2048]{1,0:T(8,128)(2,1)S(1)} %get-tuple-element.40), channel_id=1, source_target_pairs={{0,1},{1,0},{2,3},{3,2},{4,5},{5,4},{6,7},{7,6},{8,9},{9,8},{10,11... | collective-permute-start | bytes 1572872 | tf_op jit(solution)/shard_map/ppermute | solution.py:449
  36.0 10.2 %collective-permute-done.5.rest_3_ = bf16[128,1024]{1,0:T(8,128)(2,1)S(1)} collective-permute-done((bf16[128,1024]{1,0:T(8,128)(2,1)S(1)}, bf16[128,1024]{1,0:T(8,128)(2,1)S(1)}, u32[]{:S(2)}, u32[]{:S(2)}) %collective-permute-start.5) | collective-permute-done | bytes 262176 | tf_op jit(solution)/shard_map/ppermute | solution.py:449
  46.5 1.2 %collective-permute-start.13 = (bf16[256,512]{1,0:T(8,128)(2,1)S(1)}, bf16[256,512]{1,0:T(8,128)(2,1)S(1)}, u32[]{:S(2)}, u32[]{:S(2)}) collective-permute-start(bf16[256,512]{1,0:T(8,128)(2,1)S(1)} %collective-permute-done.12.rest_9_.rest_4_), channel_id=1, source_target_pairs={{0,4},{8,12},{16,20},{24,28},{4,0},{12,8},{20,16},{28,24},{1,5},{9... | collective-permute-start | bytes 786440 | tf_op jit(solution)/shard_map/ppermute | solution.py:470
  48.9 5.5 %collective-permute-done.15.rest_12_.rest_7_ = bf16[256,512]{1,0:T(8,128)(2,1)S(1)} collective-permute-done((bf16[256,512]{1,0:T(8,128)(2,1)S(1)}, bf16[256,512]{1,0:T(8,128)(2,1)S(1)}, u32[]{:S(2)}, u32[]{:S(2)}) %collective-permute-start.15) | collective-permute-done | bytes 262176 | tf_op jit(solution)/shard_map/ppermute | solution.py:470
  54.4 5.6 %collective-permute-done.13.rest_10_.rest_5_ = bf16[256,512]{1,0:T(8,128)(2,1)S(1)} collective-permute-done((bf16[256,512]{1,0:T(8,128)(2,1)S(1)}, bf16[256,512]{1,0:T(8,128)(2,1)S(1)}, u32[]{:S(2)}, u32[]{:S(2)}) %collective-permute-start.13) | collective-permute-done | bytes 262176 | tf_op jit(solution)/shard_map/ppermute | solution.py:470
  60.0 1.9 %values_part.1 = (f32[2,128,512]{2,1,0:T(8,128)S(1)}, f32[2,128,512]{2,1,0:T(8,128)S(1)}) custom-call(s32[24]{0:T(128)S(1)} %dynamic-slice_bitcast_fusion.idx_ref, bf16[128,2048]{1,0:T(8,128)(2,1)S(1)} %get-tuple-element.36.rest_0_, bf16[128,2048]{1,0:T(8,128)(2,1)S(1)} %collective-permute-done.3.rest_1_, ...), custom_call_target="tpu_custom_call" | custom-call | flops 1073741824 | bytes 8388608 | tf_op jit(solution)/shard_map/values_part/pallas_call | solution.py:340
  62.8 1.4 %collective-permute-done.16 = f32[2,128,512]{2,1,0:T(8,128)S(1)} collective-permute-done((f32[2,128,512]{2,1,0:T(8,128)S(1)}, f32[2,128,512]{2,1,0:T(8,128)S(1)}, u32[]{:S(2)}, u32[]{:S(2)}) %collective-permute-start.16) | collective-permute-done | bytes 524320 | tf_op jit(solution)/shard_map/ppermute | solution.py:449
  64.2 1.2 %collective-permute-start.17 = (bf16[2,128,512]{2,1,0:T(8,128)(2,1)S(1)}, bf16[2,128,512]{2,1,0:T(8,128)(2,1)S(1)}, u32[]{:S(2)}, u32[]{:S(2)}) collective-permute-start(bf16[2,128,512]{2,1,0:T(8,128)(2,1)S(1)} %get-tuple-element.66), channel_id=1, source_target_pairs={{0,2},{1,3},{2,0},{3,1},{4,6},{5,7},{6,4},{7,5},{8,10},{9,11},{10,... | collective-permute-start | bytes 786440 | tf_op jit(solution)/shard_map/ppermute | solution.py:449
  65.5 2.1 %weight_grad_part.1 = (bf16[256,512]{1,0:T(8,128)(2,1)S(1)}, bf16[256,512]{1,0:T(8,128)(2,1)S(1)}, bf16[256,512]{1,0:T(8,128)(2,1)S(1)}, bf16[256,512]{1,0:T(8,1...) custom-call(s32[24]{0:T(128)S(1)} %dynamic-slice_bitcast_fusion.idx_, ...), custom_call_target="tpu_custom_call" | custom-call | flops 1073741824 | bytes 7340032 | tf_op jit(solution)/shard_map/weight_grad_part/pallas_call | solution.py:377
  67.8 3.9 %collective-permute-done.17 = bf16[2,128,512]{2,1,0:T(8,128)(2,1)S(1)} collective-permute-done((bf16[2,128,512]{2,1,0:T(8,128)(2,1)S(1)}, bf16[2,128,512]{2,1,0:T(8,128)(2,1)S(1)}, u32[]{:S(2)}, u32[]{:S(2)}) %collective-permute-start.17) | collective-permute-done | bytes 262176 | tf_op jit(solution)/shard_map/ppermute | solution.py:449
  71.9 1.3 %collective-permute-start.18 = (bf16[2,128,512]{2,1,0:T(8,128)(2,1)S(1)}, bf16[2,128,512]{2,1,0:T(8,128)(2,1)S(1)}, u32[]{:S(2)}, u32[]{:S(2)}) collective-permute-start(bf16[2,128,512]{2,1,0:T(8,128)(2,1)S(1)} %add_convert_fusion.1.v0_ref), channel_id=1, source_target_pairs={{0,1},{1,0},{2,3},{3,2},{4,5},{5,4},{6,7},{7,6},{8,9},{9,8},{10,11... | collective-permute-start | bytes 786440 | tf_op jit(solution)/shard_map/ppermute | solution.py:449
  74.9 2.4 %collective-permute-start.27 = (bf16[256,512]{1,0:T(8,128)(2,1)S(1)}, bf16[256,512]{1,0:T(8,128)(2,1)S(1)}, u32[]{:S(2)}, u32[]{:S(2)}) collective-permute-start(bf16[256,512]{1,0:T(8,128)(2,1)S(1)} %fusion.3), channel_id=1, source_target_pairs={{0,16},{4,20},{16,24},{20,28},{24,8},{28,12},{8,0},{12,4},{1,17},{... | collective-permute-start | bytes 786440 | tf_op jit(solution)/shard_map/ppermute | solution.py:467
  77.4 6.4 %scores_dq_dk.1 = (bf16[128,4096]{1,0:T(8,128)(2,1)}, f32[2,128,512]{2,1,0:T(8,128)S(1)}, f32[2,128,512]{2,1,0:T(8,128)S(1)}) custom-call(s32[24]{0:T(128)S(1)} %dynamic-slice_bitcast_fusion.idx_ref, bf16[128,4096]{1,0:T(8,128)(2,1)S(1)} %bitcast.41, bf16[128,4096]{1,0:T(8,128)(2,1)S(1)} %bitcast.43, f32[32,128]{1,0:T(8,128)S(1)} %get-tuple-element.35.lse_ref, ...), custom_call_target="tpu_custom_call" | custom-call | flops 1610612736 | bytes 10485760 | tf_op jit(solution)/shard_map/scores_dq_dk/pallas_call | solution.py:293
  85.0 1.8 %collective-permute-done.30 = bf16[256,512]{1,0:T(8,128)(2,1)S(1)} collective-permute-done((bf16[256,512]{1,0:T(8,128)(2,1)S(1)}, bf16[256,512]{1,0:T(8,128)(2,1)S(1)}, u32[]{:S(2)}, u32[]{:S(2)}) %collective-permute-start.30) | collective-permute-done | bytes 262176 | tf_op jit(solution)/shard_map/ppermute | solution.py:470
  86.8 1.2 %collective-permute-start.31 = (bf16[256,512]{1,0:T(8,128)(2,1)S(1)}, bf16[256,512]{1,0:T(8,128)(2,1)S(1)}, u32[]{:S(2)}, u32[]{:S(2)}) collective-permute-start(bf16[256,512]{1,0:T(8,128)(2,1)S(1)} %fusion), channel_id=1, source_target_pairs={{16,0},{20,4},{24,16},{28,20},{8,24},{12,28},{0,8},{4,12},{17,1},{... | collective-permute-start | bytes 786440 | tf_op jit(solution)/shard_map/ppermute | solution.py:467
  89.4 2.0 %input_grad_part.1 = (bf16[128,2048]{1,0:T(8,128)(2,1)S(1)}, bf16[128,2048]{1,0:T(8,128)(2,1)S(1)}, bf16[128,2048]{1,0:T(8,128)(2,1)S(1)}, bf16[128,2048]{1,0:T(8,128)(2,1)S(1)}) custom-call(s32[24]{0:T(128)S(1)} %dynamic-slice_bitcast_fusion.idx_ref, bf16[2,128,512]{2,1,0:T(8,128)(2,1)S(1)} %add_convert_fusion.g0.rest_5_, ...), custom_call_target="tpu_custom_call" | custom-call | flops 1073741824 | bytes 5242880 | tf_op jit(solution)/shard_map/input_grad_part/pallas_call | solution.py:416
  92.5 2.3 %collective-permute-start.23 = (bf16[128,2048]{1,0:T(8,128)(2,1)S(1)}, bf16[128,2048]{1,0:T(8,128)(2,1)S(1)}, u32[]{:S(2)}, u32[]{:S(2)}) collective-permute-start(bf16[128,2048]{1,0:T(8,128)(2,1)S(1)} %get-tuple-element.55), channel_id=1, source_target_pairs={{0,1},{1,0},{2,3},{3,2},{4,5},{5,4},{6,7},{7,6},{8,9},{9,8},{10,11... | collective-permute-start | bytes 1572872 | tf_op jit(solution)/shard_map/ppermute | solution.py:449
  95.2 1.2 %collective-permute-start.20 = (bf16[128,512]{1,0:T(8,128)(2,1)S(1)}, bf16[128,512]{1,0:T(8,128)(2,1)S(1)}, u32[]{:S(2)}, u32[]{:S(2)}) collective-permute-start(bf16[128,512]{1,0:T(8,128)(2,1)S(1)} %fusion.9), channel_id=1, source_target_pairs={{0,2},{1,3},{2,0},{3,1},{4,6},{5,7},{6,4},{7,5},{8,10},{9,11},{10,... | collective-permute-start | bytes 393224 | tf_op jit(solution)/shard_map/ppermute | solution.py:449
  96.4 5.2 %collective-permute-done.29 = bf16[256,512]{1,0:T(8,128)(2,1)S(1)} collective-permute-done((bf16[256,512]{1,0:T(8,128)(2,1)S(1)}, bf16[256,512]{1,0:T(8,128)(2,1)S(1)}, u32[]{:S(2)}, u32[]{:S(2)}) %collective-permute-start.29) | collective-permute-done | bytes 262176 | tf_op jit(solution)/shard_map/ppermute | solution.py:467
  103.1 14.7 %collective-permute-done.24.rest_3_ = bf16[128,2048]{1,0:T(8,128)(2,1)S(1)} collective-permute-done((bf16[128,2048]{1,0:T(8,128)(2,1)S(1)}, bf16[128,2048]{1,0:T(8,128)(2,1)S(1)}, u32[]{:S(2)}, u32[]{:S(2)}) %collective-permute-start.24) | collective-permute-done | bytes 524320 | tf_op jit(solution)/shard_map/ppermute | solution.py:449
  117.7 2.5 %join_columns.1 = bf16[128,8192]{1,0:T(8,128)(2,1)} custom-call(s32[24]{0:T(128)S(1)} %dynamic-slice_bitcast_fusion.idx_ref, bf16[128,2048]{1,0:T(8,128)(2,1)S(1)} %get-tuple-element.53.rest_0_, bf16[128,2048]{1,0:T(8,128)(2,1)S(1)} %collective-permute-done.22.rest_1_, bf16[128,2048]{1,0:T(8,128)(2,1)S(1)} %collective-permute-done.23.rest_2_, ...), custom_call_target="tpu_custom_call" | custom-call | bytes 4194304 | tf_op jit(solution)/shard_map/join_columns/pallas_call | solution.py:119
  (64 shorter events, 17.3 us)
Async XLA Ops:
  1.6 5.6 %collective-permute-start = (bf16[144,512]{1,0:T(8,128)(2,1)S(1)}, bf16[144,512]{1,0:T(8,128)(2,1)S(1)}, u32[]{:S(2)}, u32[]{:S(2)}) collective-permute-start(bf16[144,512]{1,0:T(8,128)(2,1)S(1)} %key_block.1.rest_0_), channel_id=1, source_target_pairs={{0,2},{1,3},{2,0},{3,1},{4,6},{5,7},{6,4},{7,5},{8,10},{9,11},{10,... | collective-permute-start | bytes 442376 | tf_op jit(solution)/shard_map/ppermute | solution.py:449
  3.7 5.5 %collective-permute-start.1 = (bf16[144,512]{1,0:T(8,128)(2,1)S(1)}, bf16[144,512]{1,0:T(8,128)(2,1)S(1)}, u32[]{:S(2)}, u32[]{:S(2)}) collective-permute-start(bf16[144,512]{1,0:T(8,128)(2,1)S(1)} %key_block.1.rest_0_), channel_id=1, source_target_pairs={{0,1},{1,0},{2,3},{3,2},{4,5},{5,4},{6,7},{7,6},{8,9},{9,8},{10,11... | collective-permute-start | bytes 442376 | tf_op jit(solution)/shard_map/ppermute | solution.py:449
  7.3 2.3 %collective-permute-start.2 = (bf16[144,512]{1,0:T(8,128)(2,1)S(1)}, bf16[144,512]{1,0:T(8,128)(2,1)S(1)}, u32[]{:S(2)}, u32[]{:S(2)}) collective-permute-start(bf16[144,512]{1,0:T(8,128)(2,1)S(1)} %collective-permute-done.rest_1_), channel_id=1, source_target_pairs={{0,1},{1,0},{2,3},{3,2},{4,5},{5,4},{6,7},{7,6},{8,9},{9,8},{10,11... | collective-permute-start | bytes 442376 | tf_op jit(solution)/shard_map/ppermute | solution.py:449
  16.9 4.2 %collective-permute-start.6 = (f32[2,128,512]{2,1,0:T(8,128)S(1)}, f32[2,128,512]{2,1,0:T(8,128)S(1)}, u32[]{:S(2)}, u32[]{:S(2)}) collective-permute-start(f32[2,128,512]{2,1,0:T(8,128)S(1)} %get-tuple-element.46), channel_id=1, source_target_pairs={{0,1},{1,0},{2,3},{3,2},{4,5},{5,4},{6,7},{7,6},{8,9},{9,8},{10,11... | collective-permute-start | bytes 1572872 | tf_op jit(solution)/shard_map/ppermute | solution.py:449
  17.4 8.1 %collective-permute-start.10 = (bf16[256,512]{1,0:T(8,128)(2,1)S(1)}, bf16[256,512]{1,0:T(8,128)(2,1)S(1)}, u32[]{:S(2)}, u32[]{:S(2)}) collective-permute-start(bf16[256,512]{1,0:T(8,128)(2,1)S(1)} %copy-done), channel_id=1, source_target_pairs={{0,16},{4,20},{16,24},{20,28},{24,8},{28,12},{8,0},{12,4},{1,17},{... | collective-permute-start | bytes 786440 | tf_op jit(solution)/shard_map/ppermute | solution.py:467
  19.9 13.5 %collective-permute-start.14 = (bf16[256,512]{1,0:T(8,128)(2,1)S(1)}, bf16[256,512]{1,0:T(8,128)(2,1)S(1)}, u32[]{:S(2)}, u32[]{:S(2)}) collective-permute-start(bf16[256,512]{1,0:T(8,128)(2,1)S(1)} %copy-done), channel_id=1, source_target_pairs={{16,0},{20,4},{24,16},{28,20},{8,24},{12,28},{0,8},{4,12},{17,1},{... | collective-permute-start | bytes 786440 | tf_op jit(solution)/shard_map/ppermute | solution.py:467
  19.9 13.5 %collective-permute-start.9 = (bf16[256,512]{1,0:T(8,128)(2,1)S(1)}, bf16[256,512]{1,0:T(8,128)(2,1)S(1)}, u32[]{:S(2)}, u32[]{:S(2)}) collective-permute-start(bf16[256,512]{1,0:T(8,128)(2,1)S(1)} %copy-done), channel_id=1, source_target_pairs={{0,4},{8,12},{16,20},{24,28},{4,0},{12,8},{20,16},{28,24},{1,5},{9... | collective-permute-start | bytes 786440 | tf_op jit(solution)/shard_map/ppermute | solution.py:470
  21.3 13.4 %collective-permute-start.7 = (bf16[2,128,512]{2,1,0:T(8,128)(2,1)S(1)}, bf16[2,128,512]{2,1,0:T(8,128)(2,1)S(1)}, u32[]{:S(2)}, u32[]{:S(2)}) collective-permute-start(bf16[2,128,512]{2,1,0:T(8,128)(2,1)S(1)} %get-tuple-element.68), channel_id=1, source_target_pairs={{0,2},{1,3},{2,0},{3,1},{4,6},{5,7},{6,4},{7,5},{8,10},{9,11},{10,... | collective-permute-start | bytes 786440 | tf_op jit(solution)/shard_map/ppermute | solution.py:449
  24.7 29.7 %collective-permute-start.3 = (bf16[128,2048]{1,0:T(8,128)(2,1)S(1)}, bf16[128,2048]{1,0:T(8,128)(2,1)S(1)}, u32[]{:S(2)}, u32[]{:S(2)}) collective-permute-start(bf16[128,2048]{1,0:T(8,128)(2,1)S(1)} %get-tuple-element.38), channel_id=1, source_target_pairs={{0,2},{1,3},{2,0},{3,1},{4,6},{5,7},{6,4},{7,5},{8,10},{9,11},{10,... | collective-permute-start | bytes 1572872 | tf_op jit(solution)/shard_map/ppermute | solution.py:449
  25.5 20.7 %collective-permute-start.5 = (bf16[128,1024]{1,0:T(8,128)(2,1)S(1)}, bf16[128,1024]{1,0:T(8,128)(2,1)S(1)}, u32[]{:S(2)}, u32[]{:S(2)}) collective-permute-start(bf16[128,1024]{1,0:T(8,128)(2,1)S(1)} %get-tuple-element.42), channel_id=1, source_target_pairs={{0,3},{1,2},{2,1},{3,0},{4,7},{5,6},{6,5},{7,4},{8,11},{9,10},{10,... | collective-permute-start | bytes 786440 | tf_op jit(solution)/shard_map/ppermute | solution.py:449
  33.4 13.1 %collective-permute-start.12 = (bf16[256,512]{1,0:T(8,128)(2,1)S(1)}, bf16[256,512]{1,0:T(8,128)(2,1)S(1)}, u32[]{:S(2)}, u32[]{:S(2)}) collective-permute-start(bf16[256,512]{1,0:T(8,128)(2,1)S(1)} %collective-permute-done.10.rest_7_.rest_2_), channel_id=1, source_target_pairs={{0,16},{4,20},{16,24},{20,28},{24,8},{28,12},{8,0},{12,4},{1,17},{... | collective-permute-start | bytes 786440 | tf_op jit(solution)/shard_map/ppermute | solution.py:467
  33.4 14.3 %collective-permute-start.11 = (bf16[256,512]{1,0:T(8,128)(2,1)S(1)}, bf16[256,512]{1,0:T(8,128)(2,1)S(1)}, u32[]{:S(2)}, u32[]{:S(2)}) collective-permute-start(bf16[256,512]{1,0:T(8,128)(2,1)S(1)} %collective-permute-done.10.rest_7_.rest_2_), channel_id=1, source_target_pairs={{0,4},{8,12},{16,20},{24,28},{4,0},{12,8},{20,16},{28,24},{1,5},{9... | collective-permute-start | bytes 786440 | tf_op jit(solution)/shard_map/ppermute | solution.py:470
  34.6 19.8 %collective-permute-start.4 = (bf16[128,2048]{1,0:T(8,128)(2,1)S(1)}, bf16[128,2048]{1,0:T(8,128)(2,1)S(1)}, u32[]{:S(2)}, u32[]{:S(2)}) collective-permute-start(bf16[128,2048]{1,0:T(8,128)(2,1)S(1)} %get-tuple-element.40), channel_id=1, source_target_pairs={{0,1},{1,0},{2,3},{3,2},{4,5},{5,4},{6,7},{7,6},{8,9},{9,8},{10,11... | collective-permute-start | bytes 1572872 | tf_op jit(solution)/shard_map/ppermute | solution.py:449
  46.2 8.2 %collective-permute-start.15 = (bf16[256,512]{1,0:T(8,128)(2,1)S(1)}, bf16[256,512]{1,0:T(8,128)(2,1)S(1)}, u32[]{:S(2)}, u32[]{:S(2)}) collective-permute-start(bf16[256,512]{1,0:T(8,128)(2,1)S(1)} %collective-permute-done.14.rest_11_.rest_6_), channel_id=1, source_target_pairs={{0,4},{8,12},{16,20},{24,28},{4,0},{12,8},{20,16},{28,24},{1,5},{9... | collective-permute-start | bytes 786440 | tf_op jit(solution)/shard_map/ppermute | solution.py:470
  46.5 13.5 %collective-permute-start.13 = (bf16[256,512]{1,0:T(8,128)(2,1)S(1)}, bf16[256,512]{1,0:T(8,128)(2,1)S(1)}, u32[]{:S(2)}, u32[]{:S(2)}) collective-permute-start(bf16[256,512]{1,0:T(8,128)(2,1)S(1)} %collective-permute-done.12.rest_9_.rest_4_), channel_id=1, source_target_pairs={{0,4},{8,12},{16,20},{24,28},{4,0},{12,8},{20,16},{28,24},{1,5},{9... | collective-permute-start | bytes 786440 | tf_op jit(solution)/shard_map/ppermute | solution.py:470
  47.7 12.3 %collective-permute-start.8 = (bf16[128,1024]{1,0:T(8,128)(2,1)S(1)}, bf16[128,1024]{1,0:T(8,128)(2,1)S(1)}, u32[]{:S(2)}, u32[]{:S(2)}) collective-permute-start(bf16[128,1024]{1,0:T(8,128)(2,1)S(1)} %get-tuple-element.47), channel_id=1, source_target_pairs={{0,3},{1,2},{2,1},{3,0},{4,7},{5,6},{6,5},{7,4},{8,11},{9,10},{10,... | collective-permute-start | bytes 786440 | tf_op jit(solution)/shard_map/ppermute | solution.py:449
  62.0 2.2 %collective-permute-start.16 = (f32[2,128,512]{2,1,0:T(8,128)S(1)}, f32[2,128,512]{2,1,0:T(8,128)S(1)}, u32[]{:S(2)}, u32[]{:S(2)}) collective-permute-start(f32[2,128,512]{2,1,0:T(8,128)S(1)} %get-tuple-element.49), channel_id=1, source_target_pairs={{0,1},{1,0},{2,3},{3,2},{4,5},{5,4},{6,7},{7,6},{8,9},{9,8},{10,11... | collective-permute-start | bytes 1572872 | tf_op jit(solution)/shard_map/ppermute | solution.py:449
  62.7 2.8 %collective-permute-start.21 = (bf16[2,128,512]{2,1,0:T(8,128)(2,1)S(1)}, bf16[2,128,512]{2,1,0:T(8,128)(2,1)S(1)}, u32[]{:S(2)}, u32[]{:S(2)}) collective-permute-start(bf16[2,128,512]{2,1,0:T(8,128)(2,1)S(1)} %add_convert_fusion.g0.rest_5_), channel_id=1, source_target_pairs={{0,1},{1,0},{2,3},{3,2},{4,5},{5,4},{6,7},{7,6},{8,9},{9,8},{10,11... | collective-permute-start | bytes 786440 | tf_op jit(solution)/shard_map/ppermute | solution.py:449
  64.2 7.6 %collective-permute-start.17 = (bf16[2,128,512]{2,1,0:T(8,128)(2,1)S(1)}, bf16[2,128,512]{2,1,0:T(8,128)(2,1)S(1)}, u32[]{:S(2)}, u32[]{:S(2)}) collective-permute-start(bf16[2,128,512]{2,1,0:T(8,128)(2,1)S(1)} %get-tuple-element.66), channel_id=1, source_target_pairs={{0,2},{1,3},{2,0},{3,1},{4,6},{5,7},{6,4},{7,5},{8,10},{9,11},{10,... | collective-permute-start | bytes 786440 | tf_op jit(solution)/shard_map/ppermute | solution.py:449
  67.6 7.3 %collective-permute-start.26 = (bf16[256,512]{1,0:T(8,128)(2,1)S(1)}, bf16[256,512]{1,0:T(8,128)(2,1)S(1)}, u32[]{:S(2)}, u32[]{:S(2)}) collective-permute-start(bf16[256,512]{1,0:T(8,128)(2,1)S(1)} %get-tuple-element.60), channel_id=1, source_target_pairs={{0,4},{8,12},{16,20},{24,28},{4,0},{12,8},{20,16},{28,24},{1,5},{9... | collective-permute-start | bytes 786440 | tf_op jit(solution)/shard_map/ppermute | solution.py:470
  71.9 5.5 %collective-permute-start.18 = (bf16[2,128,512]{2,1,0:T(8,128)(2,1)S(1)}, bf16[2,128,512]{2,1,0:T(8,128)(2,1)S(1)}, u32[]{:S(2)}, u32[]{:S(2)}) collective-permute-start(bf16[2,128,512]{2,1,0:T(8,128)(2,1)S(1)} %add_convert_fusion.1.v0_ref), channel_id=1, source_target_pairs={{0,1},{1,0},{2,3},{3,2},{4,5},{5,4},{6,7},{7,6},{8,9},{9,8},{10,11... | collective-permute-start | bytes 786440 | tf_op jit(solution)/shard_map/ppermute | solution.py:449
  73.2 14.9 %collective-permute-start.28 = (bf16[256,512]{1,0:T(8,128)(2,1)S(1)}, bf16[256,512]{1,0:T(8,128)(2,1)S(1)}, u32[]{:S(2)}, u32[]{:S(2)}) collective-permute-start(bf16[256,512]{1,0:T(8,128)(2,1)S(1)} %get-tuple-element.62), channel_id=1, source_target_pairs={{0,4},{8,12},{16,20},{24,28},{4,0},{12,8},{20,16},{28,24},{1,5},{9... | collective-permute-start | bytes 786440 | tf_op jit(solution)/shard_map/ppermute | solution.py:470
  73.4 13.3 %collective-permute-start.30 = (bf16[256,512]{1,0:T(8,128)(2,1)S(1)}, bf16[256,512]{1,0:T(8,128)(2,1)S(1)}, u32[]{:S(2)}, u32[]{:S(2)}) collective-permute-start(bf16[256,512]{1,0:T(8,128)(2,1)S(1)} %get-tuple-element.64), channel_id=1, source_target_pairs={{0,4},{8,12},{16,20},{24,28},{4,0},{12,8},{20,16},{28,24},{1,5},{9... | collective-permute-start | bytes 786440 | tf_op jit(solution)/shard_map/ppermute | solution.py:470
  74.6 17.8 %collective-permute-start.25 = (bf16[256,512]{1,0:T(8,128)(2,1)S(1)}, bf16[256,512]{1,0:T(8,128)(2,1)S(1)}, u32[]{:S(2)}, u32[]{:S(2)}) collective-permute-start(bf16[256,512]{1,0:T(8,128)(2,1)S(1)} %get-tuple-element.58), channel_id=1, source_target_pairs={{0,4},{8,12},{16,20},{24,28},{4,0},{12,8},{20,16},{28,24},{1,5},{9... | collective-permute-start | bytes 786440 | tf_op jit(solution)/shard_map/ppermute | solution.py:470
  74.9 13.1 %collective-permute-start.27 = (bf16[256,512]{1,0:T(8,128)(2,1)S(1)}, bf16[256,512]{1,0:T(8,128)(2,1)S(1)}, u32[]{:S(2)}, u32[]{:S(2)}) collective-permute-start(bf16[256,512]{1,0:T(8,128)(2,1)S(1)} %fusion.3), channel_id=1, source_target_pairs={{0,16},{4,20},{16,24},{20,28},{24,8},{28,12},{8,0},{12,4},{1,17},{... | collective-permute-start | bytes 786440 | tf_op jit(solution)/shard_map/ppermute | solution.py:467
  83.8 11.0 %collective-permute-start.19 = (f32[2,128,512]{2,1,0:T(8,128)S(1)}, f32[2,128,512]{2,1,0:T(8,128)S(1)}, u32[]{:S(2)}, u32[]{:S(2)}) collective-permute-start(f32[2,128,512]{2,1,0:T(8,128)S(1)} %get-tuple-element.52), channel_id=1, source_target_pairs={{0,1},{1,0},{2,3},{3,2},{4,5},{5,4},{6,7},{7,6},{8,9},{9,8},{10,11... | collective-permute-start | bytes 1572872 | tf_op jit(solution)/shard_map/ppermute | solution.py:449
  86.8 8.4 %collective-permute-start.31 = (bf16[256,512]{1,0:T(8,128)(2,1)S(1)}, bf16[256,512]{1,0:T(8,128)(2,1)S(1)}, u32[]{:S(2)}, u32[]{:S(2)}) collective-permute-start(bf16[256,512]{1,0:T(8,128)(2,1)S(1)} %fusion), channel_id=1, source_target_pairs={{16,0},{20,4},{24,16},{28,20},{8,24},{12,28},{0,8},{4,12},{17,1},{... | collective-permute-start | bytes 786440 | tf_op jit(solution)/shard_map/ppermute | solution.py:467
  88.2 13.4 %collective-permute-start.29 = (bf16[256,512]{1,0:T(8,128)(2,1)S(1)}, bf16[256,512]{1,0:T(8,128)(2,1)S(1)}, u32[]{:S(2)}, u32[]{:S(2)}) collective-permute-start(bf16[256,512]{1,0:T(8,128)(2,1)S(1)} %fusion.2), channel_id=1, source_target_pairs={{0,16},{4,20},{16,24},{20,28},{24,8},{28,12},{8,0},{12,4},{1,17},{... | collective-permute-start | bytes 786440 | tf_op jit(solution)/shard_map/ppermute | solution.py:467
  91.4 11.7 %collective-permute-start.22 = (bf16[128,2048]{1,0:T(8,128)(2,1)S(1)}, bf16[128,2048]{1,0:T(8,128)(2,1)S(1)}, u32[]{:S(2)}, u32[]{:S(2)}) collective-permute-start(bf16[128,2048]{1,0:T(8,128)(2,1)S(1)} %get-tuple-element.54), channel_id=1, source_target_pairs={{0,2},{1,3},{2,0},{3,1},{4,6},{5,7},{6,4},{7,5},{8,10},{9,11},{10,... | collective-permute-start | bytes 1572872 | tf_op jit(solution)/shard_map/ppermute | solution.py:449
  92.5 10.6 %collective-permute-start.23 = (bf16[128,2048]{1,0:T(8,128)(2,1)S(1)}, bf16[128,2048]{1,0:T(8,128)(2,1)S(1)}, u32[]{:S(2)}, u32[]{:S(2)}) collective-permute-start(bf16[128,2048]{1,0:T(8,128)(2,1)S(1)} %get-tuple-element.55), channel_id=1, source_target_pairs={{0,1},{1,0},{2,3},{3,2},{4,5},{5,4},{6,7},{7,6},{8,9},{9,8},{10,11... | collective-permute-start | bytes 1572872 | tf_op jit(solution)/shard_map/ppermute | solution.py:449
  94.8 22.9 %collective-permute-start.24 = (bf16[128,2048]{1,0:T(8,128)(2,1)S(1)}, bf16[128,2048]{1,0:T(8,128)(2,1)S(1)}, u32[]{:S(2)}, u32[]{:S(2)}) collective-permute-start(bf16[128,2048]{1,0:T(8,128)(2,1)S(1)} %get-tuple-element.57), channel_id=1, source_target_pairs={{0,3},{1,2},{2,1},{3,0},{4,7},{5,6},{6,5},{7,4},{8,11},{9,10},{10,... | collective-permute-start | bytes 1572872 | tf_op jit(solution)/shard_map/ppermute | solution.py:449
  95.2 25.1 %collective-permute-start.20 = (bf16[128,512]{1,0:T(8,128)(2,1)S(1)}, bf16[128,512]{1,0:T(8,128)(2,1)S(1)}, u32[]{:S(2)}, u32[]{:S(2)}) collective-permute-start(bf16[128,512]{1,0:T(8,128)(2,1)S(1)} %fusion.9), channel_id=1, source_target_pairs={{0,2},{1,3},{2,0},{3,1},{4,6},{5,7},{6,4},{7,5},{8,10},{9,11},{10,... | collective-permute-start | bytes 393224 | tf_op jit(solution)/shard_map/ppermute | solution.py:449
  (5 other events, 38.8 us)
